TPU v7x, 256 devices: a whole 4x4x8 slice. The times are simulated.
256 devices in a mesh: dp: 32 (over z, y), fsdp: 8 (over x, core).
Axes of the slice: x: 4, y: 4, z: 8, core: 2. Of those that a mesh axis runs over, the one named last changes fastest.
Arguments:
- frames: bfloat16 [8, 768, 32, 1536], P('fsdp', 'dp'), may hold values from -6 to 6
- ln_gain: float32 [1536], replicated, may hold values from 0.5 to 1.5
- w_in: bfloat16 [1536, 3072], P(('dp', 'fsdp')), may hold values from -0.15625 to 0.15625
- depth_kernel: float32 [31, 1536], replicated, may hold values from -1 to 1
- bn_scale: float32 [1536], replicated, may hold values from 0.5 to 1.5
- bn_shift: float32 [1536], replicated, may hold values from -3 to 3
- w_out: bfloat16 [1536, 1536], P(('dp', 'fsdp')), may hold values from -0.15625 to 0.15625
- lengths: int32 [8, 32, 24], P('fsdp'), may hold values from 0 to 32, as said below
- destinations: int32 [8, 32, 24], P('fsdp'), may hold values from 0 to 31, as said below
- offsets: int32 [8, 32, 24], P('fsdp'), may hold values from 0 to 224, as said below
Outputs:
- encoded: bfloat16 [8, 256, 32, 1536], P('fsdp', 'dp')
Inputs may be any that keep to these rules, and one draw needn't show every extreme that they name: lengths: live slots come first in a loader and hold half of 32 to 32 frames; 0 marks an empty slot. In each group the busiest loader has all 24 slots live, the group has 256 live utterances, and one of them has 32 frames. destinations: within a group a loader sends at most one live utterance to a device, and every device receives exactly 8 live utterances. Empty slots hold 0. offsets: multiples of 32; the 8 live utterances received by one device have distinct offsets. Empty slots hold 0.
All inputs are finite; a program needn't handle non-finite values.
Results may differ from a plain program's by a relative error of at most 0.003.
Values may be sent and summed in bfloat16 or wider, within the bound.
A program may use at most 128 MiB of HBM per device.

v0:
```python
import jax
import jax.numpy as jnp
from jax import lax
from jax.sharding import PartitionSpec as P


def conv_module(blocks, utt_lengths, ln_gain, depth_kernel, bn_scale, bn_shift, full_in, full_out):
    block_count, frames_len, feature_width = blocks.shape
    wide_rows = blocks.reshape(block_count * frames_len, feature_width).astype(jnp.float32)
    row_mean = jnp.mean(wide_rows, axis=1, keepdims=True)
    centred = wide_rows - row_mean
    row_var = jnp.mean(centred * centred, axis=1, keepdims=True)
    normed = (centred * lax.rsqrt(row_var + 1e-05) * ln_gain).astype(jnp.bfloat16)
    glu_in = jnp.dot(normed, full_in, preferred_element_type=jnp.float32)
    gated_units = glu_in[:, :feature_width] * jax.nn.sigmoid(glu_in[:, feature_width:])
    gated_units = gated_units.reshape(block_count, frames_len, feature_width)
    valid_mask = jnp.arange(frames_len, dtype=jnp.int32)[None, :] < utt_lengths[:, None]
    gated_units = jnp.where(valid_mask[:, :, None], gated_units, jnp.zeros((), gated_units.dtype))
    side_reach = (depth_kernel.shape[0] - 1) // 2
    padded = jnp.pad(gated_units, ((0, 0), (side_reach, side_reach), (0, 0)))
    convolved = padded[:, 0:frames_len, :] * depth_kernel[0]
    for kernel_tap in range(1, depth_kernel.shape[0]):
        convolved = (
            convolved
            + padded[:, kernel_tap : kernel_tap + frames_len, :] * depth_kernel[kernel_tap]
        )
    shifted = convolved * bn_scale + bn_shift
    activated = (shifted * jax.nn.sigmoid(shifted)).astype(jnp.bfloat16)
    activated = activated.reshape(block_count * frames_len, feature_width)
    mixed_out = wide_rows + jnp.dot(activated, full_out, preferred_element_type=jnp.float32)
    mixed_out = mixed_out.reshape(block_count, frames_len, feature_width)
    mixed_out = jnp.where(valid_mask[:, :, None], mixed_out, jnp.zeros((), mixed_out.dtype))
    return mixed_out.astype(jnp.bfloat16)


def shards(
    frames, ln_gain, w_in, depth_kernel, bn_scale, bn_shift, w_out, lengths, destinations, offsets
):
    dp_count = lax.axis_size("dp")
    dp_index = lax.axis_index("dp")
    tab_len = lengths[0]
    tab_dest = destinations[0]
    tab_off = offsets[0]
    slot_count = tab_len.shape[1]
    recv_count = slot_count // 3
    frame_slots = frames.shape[2]
    own_len = lax.dynamic_index_in_dim(tab_len, dp_index, 0, keepdims=False)
    own_dest = lax.dynamic_index_in_dim(tab_dest, dp_index, 0, keepdims=False)
    slot_ids = jnp.arange(slot_count, dtype=jnp.int32)
    peer_ids = jnp.arange(dp_count, dtype=jnp.int32)
    send_table = ((own_dest[None, :] == peer_ids[:, None]) & (own_len[None, :] > 0)).astype(
        jnp.int32
    )
    send_slot = jnp.sum(send_table * slot_ids[None, :], axis=1)
    send_live = jnp.sum(send_table, axis=1) > 0
    key_table = jnp.where(tab_len > 0, tab_dest * recv_count + tab_off // frame_slots, -1)
    targets = dp_index * recv_count + jnp.arange(recv_count, dtype=jnp.int32)
    pick_table = (key_table[None, :, :] == targets[:, None, None]).astype(jnp.int32)
    recv_source = jnp.sum(pick_table * peer_ids[None, :, None], axis=(1, 2))
    full_in, full_out = (
        lax.all_gather(w_in, ("dp", "fsdp"), axis=0, tiled=True),
        lax.all_gather(w_out, ("dp", "fsdp"), axis=0, tiled=True),
    )
    local_out = conv_module(
        frames[0], own_len, ln_gain, depth_kernel, bn_scale, bn_shift, full_in, full_out
    )
    chosen = jnp.take(local_out, send_slot, axis=0)
    arrived = lax.all_to_all(
        jnp.where(send_live[:, None, None], chosen, jnp.zeros((), local_out.dtype)),
        "dp",
        split_axis=0,
        concat_axis=0,
        tiled=True,
    )
    result = jnp.take(arrived, recv_source, axis=0)
    return result[None]


def solution(mesh):
    return jax.shard_map(
        shards,
        mesh=mesh,
        in_specs=(
            P("fsdp", "dp", None, None),
            P(),
            P(("dp", "fsdp"), None),
            P(),
            P(),
            P(),
            P(("dp", "fsdp"), None),
            P("fsdp", None, None),
            P("fsdp", None, None),
            P("fsdp", None, None),
        ),
        out_specs=P("fsdp", "dp", None, None),
        check_vma=False,
    )
```

profile of v0, /device:TPU:1, one launch (start us, length us, event | category | flops | bytes accessed | tf_op | source)
XLA Modules:
  0.0 397.7 jit_solution(12368897338125634990)
XLA Ops:
  6.6 0.7 all-gather.7.cloned.1.call-update
  7.3 0.7 all-gather.5.cloned.1.call-update
  8.0 2.1 convert_reduce_fusion
  10.2 2.4 fusion.67
  13.4 0.3 slice_reduce_fusion.30
  13.8 2.2 fusion.70
  16.0 115.3 %all-gather.7.cloned.1.call-done = bf16[256,6,1536]{2,1,0:T(8,128)(2,1)} async-done(((bf16[1,6,1536]{2,1,0:T(8,128)(2,1)}), bf16[256,6,1536]{2,1,0:T(8,128)(2,1)}) %all-gather.7.cloned.1.call-update) | async-done | bytes 4718608 | tf_op jit(solution)/shard_map/all_gather | solution.py:62
  131.3 8.5 %reshape.188 = bf16[1536,1536]{1,0:T(8,128)(2,1)} reshape(bf16[256,6,1536]{2,1,0:T(8,128)(2,1)} %all-gather.7.cloned.1.call-done) | data formatting | bytes 9437184
  139.8 113.5 %all-gather.5.cloned.1.call-done = bf16[256,6,3072]{2,1,0:T(8,128)(2,1)} async-done(((bf16[1,6,3072]{2,1,0:T(8,128)(2,1)}), bf16[256,6,3072]{2,1,0:T(8,128)(2,1)}) %all-gather.5.cloned.1.call-update) | async-done | bytes 9437200 | tf_op jit(solution)/shard_map/all_gather | solution.py:61
  253.2 14.2 %reshape.186 = bf16[1536,3072]{1,0:T(8,128)(2,1)} reshape(bf16[256,6,3072]{2,1,0:T(8,128)(2,1)} %all-gather.5.cloned.1.call-done) | data formatting | bytes 18874368
  267.4 10.7 %fusion.79 = f32[768,3072]{1,0:T(8,128)S(1)} fusion(bf16[768,1536]{1,0:T(8,128)(2,1)} %fusion.70, bf16[1536,3072]{1,0:T(8,128)(2,1)} %reshape.186), kind=kOutput, calls=%fused_computation.177 | convolution fusion | flops 7247757312 | bytes 21233664 | tf_op jit(solution)/shard_map/dot_general | solution.py:14
  278.1 1.2 fusion.65
  279.4 0.4 broadcast_select_fusion
  279.8 0.4 copy-done.6
  280.2 17.8 %multiply_convert_fusion = bf16[24,32,1536]{2,1,0:T(8,128)(2,1)S(1)} fusion(f32[24,32,1536]{2,1,0:T(8,128)S(1)} %broadcast_select_fusion, f32[1536]{0:T(1024)S(1)} %copy-done.6, f32[1536]{0:T(1024)S(1)} %copy-done.7, f32[1536]{0:T(1024)S(1)} %get-tuple-element.34, f32[1536]{0:T(1024)S(1)} %get-tuple-element.35, f32[1536]{0:T(1024)S(1)} %get-tuple-element.6, ...), kind=kLoop, calls=%fused_computation.109 | loop fusion | flops 80216064 | bytes 7280640 | tf_op jit(solution)/shard_map/convert_element_type | solution.py:28
  298.1 4.0 %bitcast_add_fusion = bf16[768,1536]{1,0:T(8,128)(2,1)S(1)} fusion(bf16[1,24,32,1536]{3,2,1,0:T(8,128)(2,1)S(1)} %copy-done, bf16[768,1536]{1,0:T(8,128)(2,1)S(1)} %bitcast.34, bf16[1536,1536]{1,0:T(8,128)(2,1)S(1)} %bitcast.32), kind=kOutput, calls=%fused_computation.99 | convolution fusion | flops 3627417600 | bytes 11796480 | tf_op jit(solution)/shard_map/dot_general | solution.py:30
  302.2 0.5 select_convert_fusion
  302.6 2.5 gather_fusion
  305.1 4.0 %select_select_fusion = bf16[32,32,1536]{2,1,0:T(8,128)(2,1)} fusion(bf16[32,32,1536]{2,1,0:T(8,128)(2,1)} %gather_fusion, pred[32]{0:T(512)(128)(4,1)S(1)} %get-tuple-element.38, pred[32]{0:T(512)(128)(4,1)S(1)} %get-tuple-element.39), kind=kLoop, calls=%fused_computation.110 | loop fusion | flops 3145728 | bytes 6291520 | tf_op jit(solution)/shard_map/jit(_where)/select_n | solution.py:69
  309.1 7.2 %all-to-all-start = ((bf16[32,32,1536]{2,1,0:T(8,128)(2,1)}), bf16[32,32,1536]{2,1,0:T(8,128)(2,1)}, u32[]{:S(2)}, u32[]{:S(2)}) async-start(bf16[32,32,1536]{2,1,0:T(8,128)(2,1)} %select_select_fusion), calls=%async_computation | async-start | bytes 6291456 | tf_op jit(solution)/shard_map/all_to_all | solution.py:68
  316.3 0.3 select_reduce_fusion
  316.7 70.6 %all-to-all-done = bf16[32,32,1536]{2,1,0:T(8,128)(2,1)} async-done(((bf16[32,32,1536]{2,1,0:T(8,128)(2,1)}), bf16[32,32,1536]{2,1,0:T(8,128)(2,1)}, u32[]{:S(2)}, u32[]{:S(2)}) %all-to-all-start) | async-done | bytes 3145760 | tf_op jit(solution)/shard_map/all_to_all | solution.py:68
  387.3 2.5 gather_fusion.1
  389.8 1.0 bitcast_select_fusion
  (40 shorter events, 1.1 us)
Async XLA Ops:
  6.5 7.3 %copy-start = (bf16[1,24,32,1536]{3,2,1,0:T(8,128)(2,1)S(1)}, bf16[1,24,32,1536]{3,2,1,0:T(8,128)(2,1)}, u32[]{:S(2)}) copy-start(bf16[1,24,32,1536]{3,2,1,0:T(8,128)(2,1)} %param.10) | copy-start | bytes 7077892
  6.5 6.1 %copy-start.2 = (s32[1,32,24]{1,2,0:T(8,128)S(1)}, s32[1,32,24]{1,2,0:T(8,128)}, u32[]{:S(2)}) copy-start(s32[1,32,24]{1,2,0:T(8,128)} %param.17) | copy-start | bytes 9220
  6.5 6.3 %copy-start.3 = (s32[1,32,24]{1,2,0:T(8,128)S(1)}, s32[1,32,24]{1,2,0:T(8,128)}, u32[]{:S(2)}) copy-start(s32[1,32,24]{1,2,0:T(8,128)} %param.18) | copy-start | bytes 9220
  6.5 6.7 %copy-start.1 = (f32[31,1536]{1,0:T(8,128)S(1)}, f32[31,1536]{1,0:T(8,128)}, u32[]{:S(2)}) copy-start(f32[31,1536]{1,0:T(8,128)} %param.13) | copy-start | bytes 571396
  6.5 7.3 %copy-start.5 = (f32[1536]{0:T(1024)S(1)}, f32[1536]{0:T(1024)}, u32[]{:S(2)}) copy-start(f32[1536]{0:T(1024)} %param.11) | copy-start | bytes 18436
  6.5 124.8 %all-gather.7.cloned.1.call-start = ((), (), s32[]{:S(2)}) async-start(), calls=%async_computation.2 | async-start | bytes 6316032 | tf_op jit(solution)/shard_map/all_gather | solution.py:62
  7.3 245.9 %all-gather.5.cloned.1.call-start = ((), (), s32[]{:S(2)}) async-start(), calls=%async_computation.1 | async-start | bytes 12632064 | tf_op jit(solution)/shard_map/all_gather | solution.py:61
  279.4 18.7 %slice-start = ((s8[4718592]{0:T(1024)(128)(4,1)}), s8[4194304]{0:T(1024)(128)(4,1)S(1)}, s32[]{:S(2)}) async-start(s8[4718592]{0:T(1024)(128)(4,1)} %bitcast.31), calls=%async_computation.3 | async-start | bytes 8388608
  279.4 0.8 copy-start.6
  279.4 0.9 copy-start.7
  279.4 18.7 %slice-start.1 = ((s8[4718592]{0:T(1024)(128)(4,1)}), s8[524288]{0:T(1024)(128)(4,1)S(1)}, s32[]{:S(2)}) async-start(s8[4718592]{0:T(1024)(128)(4,1)} %bitcast.31), calls=%async_computation.4 | async-start | bytes 1048576
  309.1 7.2 %copy-start.4 = (s32[1,32,24]{1,2,0:T(8,128)S(1)}, s32[1,32,24]{1,2,0:T(8,128)}, u32[]{:S(2)}) copy-start(s32[1,32,24]{1,2,0:T(8,128)} %param.19) | copy-start | bytes 9220
  309.1 78.2 %all-to-all-start = ((bf16[32,32,1536]{2,1,0:T(8,128)(2,1)}), bf16[32,32,1536]{2,1,0:T(8,128)(2,1)}, u32[]{:S(2)}, u32[]{:S(2)}) async-start(bf16[32,32,1536]{2,1,0:T(8,128)(2,1)} %select_select_fusion), calls=%async_computation | async-start | bytes 6291456 | tf_op jit(solution)/shard_map/all_to_all | solution.py:68
Sparse Core Ops, SparseCore 0:
  11.1 120.1 all-gather.6
  135.0 118.1 all-gather.4
where the time goes:
time: 400 us; the launch traced here: 398 us
  waiting for transfers between devices  301 us (75%)
  other arithmetic  32.1 us (8%)
  local copies, waits for them, and re-layouts  29.1 us (7%)
  matrix products  14.8 us (4%)
  between operations  13.6 us (3%)
  starting transfers between devices  7.26 us (2%)
    all_gather x1, waiting for transfers between devices, shards(): lax.all_gather(w_out, ('dp', 'fsdp'), axis=0, tiled=True)  115 us
    all_gather x1, waiting for transfers between devices, shards(): lax.all_gather(w_in, ('dp', 'fsdp'), axis=0, tiled=True)  113 us
    all_to_all x1, waiting for transfers between devices, shards(): lax.all_to_all(jnp.where(send_live[:, None, None], chosen, jnp.zeros((),...  70.6 us
    unnamed x22, local copies, waits for them, and re-layouts  23.1 us
    convert_element_type x1, other arithmetic, conv_module(): activated = (shifted * jax.nn.sigmoid(shifted)).astype(jnp.bfloat16)  17.8 us
    dot_general x1, matrix products, conv_module(): glu_in = jnp.dot(normed, full_in, preferred_element_type=jnp.float32)  10.7 us
  transfers between devices with their start and end apart: 3, of which 3 were waited for; matrix products, arithmetic and copies ran while one was open for 4% of the time, Pallas kernels for 0%

commit v1 on v0

v1 whole, which is shorter than its diff:
```python
import jax
import jax.numpy as jnp
from jax import lax
from jax.experimental import pallas as pl
from jax.experimental.pallas import tpu as pltpu
from jax.sharding import PartitionSpec as P

MESH = pl.DeviceIdType.MESH

D = 1536
KERNEL = 31
MAXLEN = 32
RSLOT = 8
NZ, NY, NX, NC = 8, 4, 4, 2
N_DP = NZ * NY
SHARD_ROWS = 6
BLOCK_ROWS = 24
CHUNK = D // NX
BLOCK_COLS = 3 * CHUNK
PAD = 16

OFFSETS = sorted(
    [(dz, dy) for dz in range(NZ) for dy in range(NY) if (dz, dy) != (0, 0)],
    key=lambda o: -(min(o[0], NZ - o[0]) * 8 + min(o[1], NY - o[1])),
)
ISSUE = (6, 8, 12, 16, 20, 26, 31)


def comm_kernel(
    chosen, wp, arr, full, parts, block,
    a2a_send, a2a_recv, part_send, part_recv, block_sem,
    zu_send, zu_recv, zd_send, zd_recv,
    yu_send, yu_recv, yd_send, yd_recv,
    xu_send, xu_recv, xd_send, xd_recv,
    core_send, core_recv,
):
    dp = lax.axis_index("dp")
    fs = lax.axis_index("fsdp")
    z, y = dp // NY, dp % NY
    x, c = fs // NC, fs % NC
    other = 1 - c

    def dev(zz, yy, xx, cc):
        return (lax.rem(zz, NZ) * NY + lax.rem(yy, NY), lax.rem(xx, NX) * NC + cc)

    barrier = pltpu.get_barrier_semaphore()
    for dz, dy in OFFSETS:
        pl.semaphore_signal(barrier, inc=1, device_id=dev(z + dz, y + dy, x, c), device_id_type=MESH)
    for k in range(1, NX * NC):
        peer = lax.rem(fs + k, NX * NC)
        pl.semaphore_signal(barrier, inc=1, device_id=(dp, peer), device_id_type=MESH)
    pl.semaphore_wait(barrier, len(OFFSETS) + NX * NC - 1)

    def remote(src, dst, send, recv, device):
        return pltpu.make_async_remote_copy(
            src_ref=src, dst_ref=dst, send_sem=send, recv_sem=recv, device_id=device, device_id_type=MESH
        )

    started = []

    def start(copy):
        copy.start()
        started.append(copy)

    def frames_until(count):
        for i in range(len(frame_copies), count):
            dz, dy = OFFSETS[i]
            target = dev(z + dz, y + dy, x, c)
            copy = remote(chosen.at[target[0]], arr.at[dp], a2a_send.at[i], a2a_recv.at[i], target)
            copy.start()
            frame_copies.append(copy)

    frame_copies = []

    slot = lax.rem(x, 2) * NC + c
    keeper = x // 2
    for t in range(NX):
        same = jnp.logical_and(x == t, keeper == c)

        @pl.when(jnp.logical_not(same))
        def _():
            remote(wp.at[t], parts.at[slot], part_send.at[t], part_recv.at[slot], (dp, t * NC + keeper)).start()

        @pl.when(same)
        def _():
            pltpu.make_async_copy(wp.at[t], parts.at[slot], block_sem.at[0]).start()

    frames_until(ISSUE[0])

    for k in range(4):
        source = c * 4 + k

        @pl.when(source != fs)
        def _():
            remote(wp.at[0], parts.at[k], part_send.at[0], part_recv.at[k], (dp, fs)).wait_recv()

        @pl.when(source == fs)
        def _():
            pltpu.make_async_copy(wp.at[0], parts.at[k], block_sem.at[0]).wait()

    row = lax.broadcasted_iota(jnp.int32, (BLOCK_ROWS, 32), 0)
    col = lax.broadcasted_iota(jnp.int32, (BLOCK_ROWS, 32), 1)
    pick = (col == (row // SHARD_ROWS) * 8 + lax.rem(row, SHARD_ROWS)).astype(jnp.bfloat16)
    block[...] = jnp.dot(
        pick, parts[...].reshape(32, BLOCK_COLS), preferred_element_type=jnp.float32
    ).astype(jnp.bfloat16)

    own = pltpu.make_async_copy(block, full.at[x, z, y, c], block_sem.at[1])
    own.start()

    up, down = dev(z + 1, y, x, c), dev(z + NZ - 1, y, x, c)

    def z_up(s):
        src = lax.rem(z + NZ - s, NZ)
        return remote(block if s == 0 else full.at[x, src, y, c], full.at[x, src, y, c], zu_send.at[s], zu_recv.at[s], up)

    def z_down(s):
        src = lax.rem(z + s, NZ)
        return remote(block if s == 0 else full.at[x, src, y, c], full.at[x, src, y, c], zd_send.at[s], zd_recv.at[s], down)

    def z_landed(s, sign):
        src = lax.rem(z + NZ + sign * (s + 1), NZ)
        recv = zu_recv if sign < 0 else zd_recv
        ref = full.at[x, src, y, c]
        return remote(ref, ref, zu_send.at[s], recv.at[s], up)

    start(z_up(0))
    start(z_down(0))
    for s in range(4):
        frames_until(ISSUE[1 + s])
        z_landed(s, -1).wait_recv()
        if s < 3:
            start(z_up(s + 1))
            z_landed(s, 1).wait_recv()
            if s < 2:
                start(z_down(s + 1))
    own.wait()

    def piece(xx, yy, half=None):
        rows = slice(None) if half is None else pl.ds(half * 4, 4)
        return full.at[lax.rem(xx, NX), rows, lax.rem(yy, NY), c]

    y_up, y_down = dev(z, y + 1, x, c), dev(z, y + NY - 1, x, c)
    x_up, x_down = dev(z, y, x + 1, c), dev(z, y, x + NX - 1, c)
    sibling = (dp, x * NC + other)

    def send(ref, s_sem, r_sem, device):
        start(remote(ref, ref, s_sem, r_sem, device))

    def landed(ref, r_sem):
        remote(ref, ref, yu_send.at[0], r_sem, sibling).wait_recv()

    def to_core(dx, j, ref):
        send(ref, core_send.at[dx * 5 + j], core_recv.at[dx * 5 + j], sibling)

    def x_start(j, ref):
        send(ref, xu_send.at[j], xu_recv.at[j], x_up)
        send(ref, xd_send.at[j], xd_recv.at[j], x_down)
        to_core(0, j, ref)

    mine = piece(x, y)
    send(mine, yu_send.at[0], yu_recv.at[0], y_up)
    send(mine, yd_send.at[0], yd_recv.at[0], y_down)
    x_start(0, mine)
    frames_until(ISSUE[5])

    landed(piece(x, y + 3), yu_recv.at[0])
    send(piece(x, y + 3, 0), yu_send.at[1], yu_recv.at[1], y_up)
    x_start(1, piece(x, y + 3))
    landed(piece(x, y + 1), yd_recv.at[0])
    send(piece(x, y + 1, 1), yd_send.at[1], yd_recv.at[1], y_down)
    x_start(2, piece(x, y + 1))
    frames_until(ISSUE[6])

    rows_of = [(0, None), (3, None), (1, None), (2, 0), (2, 1)]

    def x_landed(j, first):
        dy, half = rows_of[j]
        lo, hi = (0, 1) if half is None else (half, half)
        landed(piece(x + 3, y + dy, half), xu_recv.at[j])
        landed(piece(x + 1, y + dy, half), xd_recv.at[j])
        if half is None:
            send(piece(x + 3, y + dy, 0), xu_send.at[5 + j], xu_recv.at[5 + j], x_up)
            send(piece(x + 1, y + dy, 1), xd_send.at[5 + j], xd_recv.at[5 + j], x_down)
        elif half == 0:
            send(piece(x + 3, y + dy, 0), xu_send.at[5 + j], xu_recv.at[5 + j], x_up)
        else:
            send(piece(x + 1, y + dy, 1), xd_send.at[5 + j], xd_recv.at[5 + j], x_down)
        to_core(1, j, piece(x + 3, y + dy, half))
        to_core(2, j, piece(x + 1, y + dy, half))

    def x_far_landed(j):
        dy, half = rows_of[j]
        if half in (None, 0):
            landed(piece(x + 2, y + dy, 0), xu_recv.at[5 + j])
        if half in (None, 1):
            landed(piece(x + 2, y + dy, 1), xd_recv.at[5 + j])
        to_core(3, j, piece(x + 2, y + dy, half))

    x_landed(0, True)
    landed(piece(x, y + 2, 0), yu_recv.at[1])
    x_start(3, piece(x, y + 2, 0))
    landed(piece(x, y + 2, 1), yd_recv.at[1])
    x_start(4, piece(x, y + 2, 1))
    for j in range(1, 5):
        x_landed(j, True)
        x_far_landed(j - 1)
    x_far_landed(4)

    for dx in range(NX):
        for j in range(5):
            dy, half = rows_of[j]
            rows = slice(None) if half is None else pl.ds(half * 4, 4)
            xx = lax.rem(x + (0, 3, 1, 2)[dx], NX)
            landed(full.at[xx, rows, lax.rem(y + dy, NY), other], core_recv.at[dx * 5 + j])

    for i, (dz, dy) in enumerate(OFFSETS):
        sender = dev(z + NZ - dz, y + NY - dy, x, c)[0]
        landed(arr.at[sender], a2a_recv.at[i])

    for t in range(NX):
        same = jnp.logical_and(x == t, keeper == c)

        @pl.when(jnp.logical_not(same))
        def _():
            remote(wp.at[t], parts.at[0], part_send.at[t], part_recv.at[0], sibling).wait_send()

    for copy in started + frame_copies:
        copy.wait_send()


def communicate(chosen, wp):
    dma = pltpu.SemaphoreType.DMA
    return pl.pallas_call(
        comm_kernel,
        out_shape=(
            jax.ShapeDtypeStruct((N_DP, MAXLEN, D), jnp.bfloat16),
            jax.ShapeDtypeStruct((NX, NZ, NY, NC, BLOCK_ROWS, BLOCK_COLS), jnp.bfloat16),
        ),
        in_specs=[pl.BlockSpec(memory_space=pl.ANY)] * 2,
        out_specs=(pl.BlockSpec(memory_space=pl.ANY), pl.BlockSpec(memory_space=pl.ANY)),
        scratch_shapes=[
            pltpu.VMEM((4, 8, BLOCK_COLS), jnp.bfloat16),
            pltpu.VMEM((BLOCK_ROWS, BLOCK_COLS), jnp.bfloat16),
            dma((31,)), dma((31,)), dma((4,)), dma((4,)), dma((2,)),
            dma((4,)), dma((4,)), dma((3,)), dma((3,)),
            dma((2,)), dma((2,)), dma((2,)), dma((2,)),
            dma((10,)), dma((10,)), dma((10,)), dma((10,)),
            dma((20,)), dma((20,)),
        ],
        compiler_params=pltpu.CompilerParams(collective_id=0, has_side_effects=True),
        name="exchange",
    )(chosen, wp)


def module_kernel(
    source, length, me, arr, chosen, full, gain, taps, scale, shift, out,
    xbuf, wbuf, normed, hidden, window, act, x_sem, w_sem,
):
    for r in range(RSLOT):
        @pl.when(source[r] != me[0])
        def _():
            pltpu.make_async_copy(arr.at[source[r]], xbuf.at[r], x_sem.at[r]).start()

        @pl.when(source[r] == me[0])
        def _():
            pltpu.make_async_copy(chosen.at[source[r]], xbuf.at[r], x_sem.at[r]).start()
    loads = [pltpu.make_async_copy(full.at[i], wbuf.at[i], w_sem.at[i]) for i in range(NX)]
    for load in loads:
        load.start()

    window[...] = jnp.zeros_like(window)
    for r in range(RSLOT):
        pltpu.make_async_copy(arr.at[0], xbuf.at[r], x_sem.at[r]).wait()

    def norm(r, carry):
        wide = xbuf[r].astype(jnp.float32)
        mean = jnp.mean(wide, axis=1, keepdims=True)
        centred = wide - mean
        var = jnp.mean(centred * centred, axis=1, keepdims=True)
        normed[pl.ds(pl.multiple_of(r * MAXLEN, MAXLEN), MAXLEN), :] = (
            centred * lax.rsqrt(var + 1e-05) * gain[...]
        ).astype(jnp.bfloat16)
        return carry

    lax.fori_loop(0, RSLOT, norm, 0)

    step_ids = lax.broadcasted_iota(jnp.int32, (MAXLEN, 128), 0)
    for i in range(NX):
        loads[i].wait()
        hidden[...] = jnp.dot(normed[...], wbuf[i, :, 0 : 2 * CHUNK], preferred_element_type=jnp.float32)
        for b in range(CHUNK // 128):
            lane = slice(i * CHUNK + b * 128, i * CHUNK + b * 128 + 128)
            tap = [jnp.broadcast_to(taps[k : k + 1, lane], (8, 128)) for k in range(KERNEL)]
            mul = jnp.broadcast_to(scale[:, lane], (16, 128))
            add = jnp.broadcast_to(shift[:, lane], (16, 128))

            def conv(r, carry):
                base = pl.multiple_of(r * MAXLEN, MAXLEN)
                value = hidden[pl.ds(base, MAXLEN), b * 128 : b * 128 + 128]
                gate = hidden[pl.ds(base, MAXLEN), CHUNK + b * 128 : CHUNK + b * 128 + 128]
                gated = jnp.where(step_ids < length[r], value * jax.nn.sigmoid(gate), 0.0)
                window[r, PAD : PAD + MAXLEN, :] = gated
                for pair in range(2):
                    tiles = []
                    for t in (2 * pair, 2 * pair + 1):
                        total = None
                        for k in range(KERNEL):
                            first = 8 * t + k - 15
                            if first + 7 < 0 or first > MAXLEN - 1:
                                continue
                            term = window[r, PAD + first : PAD + first + 8, :] * tap[k]
                            total = term if total is None else total + term
                        tiles.append(total)
                    s = jnp.concatenate(tiles, axis=0) * mul + add
                    act[pl.ds(pl.multiple_of(base + 16 * pair, 16), 16), lane] = (
                        s * jax.nn.sigmoid(s)
                    ).astype(jnp.bfloat16)
                return carry

            lax.fori_loop(0, RSLOT, conv, 0)

    for i in range(NX):
        lane = slice(i * CHUNK, (i + 1) * CHUNK)
        hidden[:, 0:CHUNK] = jnp.dot(
            act[...], wbuf[i, :, 2 * CHUNK : 3 * CHUNK], preferred_element_type=jnp.float32
        )
        ids = lax.broadcasted_iota(jnp.int32, (MAXLEN, CHUNK), 0)

        def close(r, carry):
            mixed = xbuf[r, :, lane].astype(jnp.float32) + hidden[
                pl.ds(pl.multiple_of(r * MAXLEN, MAXLEN), MAXLEN), 0:CHUNK
            ]
            out[r, :, lane] = jnp.where(ids < length[r], mixed, 0.0).astype(jnp.bfloat16)
            return carry

        lax.fori_loop(0, RSLOT, close, 0)


def conv_module(source, length, me, arr, chosen, full, gain, taps, scale, shift):
    smem = pl.BlockSpec(memory_space=pltpu.SMEM)
    vmem = pl.BlockSpec(memory_space=pltpu.VMEM)
    hbm = pl.BlockSpec(memory_space=pl.ANY)
    return pl.pallas_call(
        module_kernel,
        out_shape=jax.ShapeDtypeStruct((RSLOT, MAXLEN, D), jnp.bfloat16),
        in_specs=[smem, smem, smem, hbm, hbm, hbm, vmem, vmem, vmem, vmem],
        out_specs=vmem,
        scratch_shapes=[
            pltpu.VMEM((RSLOT, MAXLEN, D), jnp.bfloat16),
            pltpu.VMEM((NX, D, BLOCK_COLS), jnp.bfloat16),
            pltpu.VMEM((RSLOT * MAXLEN, D), jnp.bfloat16),
            pltpu.VMEM((RSLOT * MAXLEN, 2 * CHUNK), jnp.float32),
            pltpu.VMEM((RSLOT, MAXLEN + 2 * PAD, 128), jnp.float32),
            pltpu.VMEM((RSLOT * MAXLEN, D), jnp.bfloat16),
            pltpu.SemaphoreType.DMA((RSLOT,)),
            pltpu.SemaphoreType.DMA((NX,)),
        ],
        compiler_params=pltpu.CompilerParams(vmem_limit_bytes=48 * 1024 * 1024),
        name="conv_module",
    )(source, length, me, arr, chosen, full, gain, taps, scale, shift)


def shards(frames, ln_gain, w_in, depth_kernel, bn_scale, bn_shift, w_out, lengths, destinations, offsets):
    dp = lax.axis_index("dp")
    tab_len, tab_dest, tab_off = lengths[0], destinations[0], offsets[0]
    slots = tab_len.shape[1]
    own_len = lax.dynamic_index_in_dim(tab_len, dp, 0, keepdims=False)
    own_dest = lax.dynamic_index_in_dim(tab_dest, dp, 0, keepdims=False)
    peers = jnp.arange(N_DP, dtype=jnp.int32)
    sends = ((own_dest[None, :] == peers[:, None]) & (own_len[None, :] > 0)).astype(jnp.int32)
    send_slot = jnp.sum(sends * jnp.arange(slots, dtype=jnp.int32)[None, :], axis=1)
    chosen = jnp.take(frames[0], send_slot, axis=0)

    key = jnp.where(tab_len > 0, tab_dest * RSLOT + tab_off // MAXLEN, -1)
    targets = dp * RSLOT + jnp.arange(RSLOT, dtype=jnp.int32)
    match = (key[None, :, :] == targets[:, None, None]).astype(jnp.int32)
    source = jnp.sum(match * peers[None, :, None], axis=(1, 2))
    length = jnp.sum(match * tab_len[None, :, :], axis=(1, 2))

    w_rows = jnp.concatenate(
        [w_in.reshape(SHARD_ROWS, 2, NX, CHUNK), w_out.reshape(SHARD_ROWS, 1, NX, CHUNK)], axis=1
    )
    wp = jnp.transpose(w_rows, (2, 0, 1, 3)).reshape(NX, SHARD_ROWS, BLOCK_COLS)
    wp = jnp.pad(wp, ((0, 0), (0, 8 - SHARD_ROWS), (0, 0)))

    arr, full = communicate(chosen, wp)
    out = conv_module(
        source, length, dp.reshape(1).astype(jnp.int32), arr, chosen,
        full.reshape(NX, D, BLOCK_COLS), ln_gain[None], depth_kernel, bn_scale[None], bn_shift[None],
    )
    return out[None]


def solution(mesh):
    return jax.shard_map(
        shards,
        mesh=mesh,
        in_specs=(
            P("fsdp", "dp", None, None),
            P(),
            P(("dp", "fsdp"), None),
            P(),
            P(),
            P(),
            P(("dp", "fsdp"), None),
            P("fsdp", None, None),
            P("fsdp", None, None),
            P("fsdp", None, None),
        ),
        out_specs=P("fsdp", "dp", None, None),
        check_vma=False,
    )
```

time: 400 us -> 184 us (0.46)
  waiting for transfers between devices: 301 us -> 0 us
  Pallas kernels: 0 us -> 164 us
  other arithmetic: 32.1 us -> 6.9 us
  local copies, waits for them, and re-layouts: 29.1 us -> 11.3 us
  matrix products: 14.8 us -> 0 us
  between operations: 13.6 us -> 0.08 us
  starting transfers between devices: 7.26 us -> 0 us
    all_gather x2 -> x0, waiting for transfers between devices: 229 us -> none  [the longest x1 115 us: shards(): lax.all_gather(w_out, ('dp', 'fsdp'), axis=0, tiled=True)]
    pallas_call x0 -> x2, Pallas kernels: none -> 164 us  [the longest x1 147 us: communicate(): pl.pallas_call(comm_kernel, out_shape=(jax.ShapeDtypeStruct((N_DP, MAXLEN...]
    all_to_all x1 -> x0, waiting for transfers between devices: 70.6 us -> none  [shards(): lax.all_to_all(jnp.where(send_live[:, None, None], chosen, jnp.zeros((),...]
    convert_element_type x3 -> x0, other arithmetic: 20.5 us -> none  [the longest x1 17.8 us: conv_module(): activated = (shifted * jax.nn.sigmoid(shifted)).astype(jnp.bfloat16)]
    unnamed x22 -> x6, local copies, waits for them, and re-layouts: 23.1 us -> 3.55 us
    dot_general x2 -> x0, matrix products: 14.8 us -> none  [the longest x1 10.7 us: conv_module(): glu_in = jnp.dot(normed, full_in, preferred_element_type=jnp.float32)]
    all_to_all x1 -> x0, starting transfers between devices: 7.19 us -> none  [shards(): lax.all_to_all(jnp.where(send_live[:, None, None], chosen, jnp.zeros((),...]
  transfers between devices with their start and end apart: 3 -> 0, of which waited for: 3 -> 0; matrix products, arithmetic and copies ran while one was open for 4% -> 0% of each run, Pallas kernels for 0% -> 0%
where the time goes in v1:
time: 184 us; the launch traced here: 183 us
  Pallas kernels  164 us (89%)
  local copies, waits for them, and re-layouts  11.3 us (6%)
  other arithmetic  6.9 us (4%)
    pallas_call x1, Pallas kernels, communicate(): pl.pallas_call(comm_kernel, out_shape=(jax.ShapeDtypeStruct((N_DP, MAXLEN...  147 us
    pallas_call x1, Pallas kernels, conv_module(): pl.pallas_call(module_kernel, out_shape=jax.ShapeDtypeStruct((RSLOT, MAXL...  17.6 us
    select_n x2, other arithmetic, shards(): chosen = jnp.take(frames[0], send_slot, axis=0)  3.9 us

profile of v1, /device:TPU:1, one launch (start us, length us, event | category | flops | bytes accessed | tf_op | source)
XLA Modules:
  0.0 182.6 jit_solution(11634992787021696906)
XLA Ops:
  0.0 0.0 copy-start
  0.0 1.7 copy-done
  1.7 0.9 dynamic-slice_reduce_fusion
  2.6 0.9 fusion.8
  3.4 0.1 select_reduce_fusion
  3.6 0.7 broadcast_in_dim.33.gain
  4.3 0.7 broadcast_in_dim.34.scale
  5.0 0.7 broadcast_in_dim.35.shift
  5.7 0.8 fusion.5
  6.4 1.2 fusion.1
  7.6 0.8 reshape.50
  8.5 0.8 reshape.62
  9.2 0.1 maximum_bitcast_fusion
  9.3 0.1 reshape.52
  9.4 0.6 pad.4.wp
  10.1 2.4 %gather_fusion = bf16[32,32,1536]{2,1,0:T(8,128)(2,1)} fusion(bf16[24,32,1536]{2,1,0:T(8,128)(2,1)S(1)} %bitcast.15, s32[1024]{0:T(1024)S(1)} %pad_clamp_fusion), kind=kCustom, calls=%fused_computation | custom fusion | bytes 6291584 | tf_op jit(solution)/shard_map/jit(_take)/gather | solution.py:373
  12.4 3.9 %broadcast_select_fusion.chosen = bf16[32,32,1536]{2,1,0:T(8,128)(2,1)} fusion(bf16[32,32,1536]{2,1,0:T(8,128)(2,1)} %gather_fusion, pred[32]{0:T(512)(128)(4,1)S(1)} %compare_and_fusion), kind=kLoop, calls=%fused_computation.1 | loop fusion | flops 1572864 | bytes 6291488 | tf_op jit(solution)/shard_map/jit(_take)/select_n | solution.py:373
  16.3 0.0 copy-start.2
  16.3 146.8 %exchange.1 = (bf16[32,32,1536]{2,1,0:T(8,128)(2,1)}, bf16[4,8,4,2,24,1152]{5,4,3,2,1,0:T(8,128)(2,1)}) custom-call(bf16[32,32,1536]{2,1,0:T(8,128)(2,1)} %broadcast_select_fusion.chosen, bf16[4,8,1152]{2,1,0:T(8,128)(2,1)} %pad.4.wp), custom_call_target="tpu_custom_call" | custom-call | tf_op jit(solution)/shard_map/exchange/pallas_call | solution.py:234
  163.2 0.0 copy-done.2
  163.2 0.0 copy-start.1
  163.2 1.9 %copy-done.1 = bf16[32,32,1536]{2,1,0:T(8,128)(2,1)S(1)} copy-done((bf16[32,32,1536]{2,1,0:T(8,128)(2,1)S(1)}, bf16[32,32,1536]{2,1,0:T(8,128)(2,1)}, u32[]{:S(2)}) %copy-start.1) | copy-done | bytes 3145752
  165.1 17.6 %conv_module.1 = bf16[8,32,1536]{2,1,0:T(8,128)(2,1)} custom-call(s32[8]{0:T(128)S(1)} %get-tuple-element.10.source, s32[8]{0:T(128)S(1)} %get-tuple-element.9.length, s32[1]{0:T(128)} %bitcast.2.me, bf16[32,32,1536]{2,1,0:T(8,128)(2,1)S(1)} %copy-done.1, bf16[32,32,1536]{2,1,0:T(8,128)(2,1)} %broadcast_select_fusion.chosen, ...), custom_call_target="tpu_custom_call" | custom-call | tf_op jit(solution)/shard_map/conv_module/pallas_call | solution.py:344
  (6 shorter events, 0.1 us)
Async XLA Ops:
  0.0 1.7 copy-start
  16.3 146.9 %copy-start.2 = (f32[31,1536]{1,0:T(8,128)S(1)}, f32[31,1536]{1,0:T(8,128)}, u32[]{:S(2)}) copy-start(f32[31,1536]{1,0:T(8,128)} %taps.1) | copy-start | bytes 571396
  163.2 1.9 %copy-start.1 = (bf16[32,32,1536]{2,1,0:T(8,128)(2,1)S(1)}, bf16[32,32,1536]{2,1,0:T(8,128)(2,1)}, u32[]{:S(2)}) copy-start(bf16[32,32,1536]{2,1,0:T(8,128)(2,1)} %get-tuple-element.7.arr) | copy-start | bytes 9437188

commit v2 on v1

v2 whole, which is shorter than its diff:
```python
import jax
import jax.numpy as jnp
from jax import lax
from jax.experimental import pallas as pl
from jax.experimental.pallas import tpu as pltpu
from jax.sharding import PartitionSpec as P

MESH = pl.DeviceIdType.MESH

D = 1536
KERNEL = 31
MAXLEN = 32
RSLOT = 8
NZ, NY, NX, NC = 8, 4, 4, 2
N_DP = NZ * NY
SHARD_ROWS = 6
BLOCK_ROWS = 24
CHUNK = D // NX
BLOCK_COLS = 3 * CHUNK
PAD = 16

HALF = MAXLEN // 2
PIECES = [(3, None), (1, None), (2, 0), (2, 1)]
ARRIVALS = [0, 7, 1, 6, 2, 5, 3, 4]
UP_FORWARD = (0, 1, 2, 3)


def comm_kernel(
    codes, send_slot, frames, w_in, w_out, out, full,
    wp, parts, block, staged,
    far0, far1, up2_0, up2_1, dn2_0, dn2_1, up3_0, up3_1, dn3_0, dn3_1, up4_0, up4_1, dn4_0, dn4_1, last0, last1,
    mu3_0, mu3_1, md3_0, md3_1, mu4_0, mu4_1, md4_0, md4_1,
    fy_send, fy_recv, fz_send, fz_recv,
    part_send, part_recv, local_sem,
    zu_send, zu_recv, zd_send, zd_recv,
    yu_send, yu_recv, yd_send, yd_recv,
    xu_send, xu_recv, xd_send, xd_recv,
    core_send, core_recv,
):
    dp = lax.axis_index("dp")
    fs = lax.axis_index("fsdp")
    z, y = dp // NY, dp % NY
    x, c = fs // NC, fs % NC
    other = 1 - c
    far, last = (far0, far1), (last0, last1)
    two = ((up2_0, up2_1), (dn2_0, dn2_1))
    three = ((up3_0, up3_1), (dn3_0, dn3_1))
    four = ((up4_0, up4_1), (dn4_0, dn4_1))
    merged3 = ((mu3_0, mu3_1), (md3_0, md3_1))
    merged4 = ((mu4_0, mu4_1), (md4_0, md4_1))

    def dev(zz, yy, xx, cc):
        return (lax.rem(zz, NZ) * NY + lax.rem(yy, NY), lax.rem(xx, NX) * NC + cc)

    sibling = (dp, x * NC + other)
    z_next = (dev(z + 1, y, x, c), dev(z + NZ - 1, y, x, c))
    y_next = (dev(z, y + 1, x, c), dev(z, y + NY - 1, x, c))
    x_next = (dev(z, y, x + 1, c), dev(z, y, x + NX - 1, c))

    barrier = pltpu.get_barrier_semaphore()

    def greet(device):
        pl.semaphore_signal(barrier, inc=1, device_id=device, device_id_type=MESH)

    for k in range(1, NX * NC):
        greet((dp, lax.rem(fs + k, NX * NC)))
    for k in range(1, NY):
        greet(dev(z, y + k, x, c))
    for device in z_next:
        greet(device)

    def remote(src, dst, send, recv, device):
        return pltpu.make_async_remote_copy(
            src_ref=src, dst_ref=dst, send_sem=send, recv_sem=recv, device_id=device, device_id_type=MESH
        )

    started = []

    def start(src, dst, s_sem, r_sem, device):
        copy = remote(src, dst, s_sem, r_sem, device)
        copy.start()
        started.append(copy)

    def landed(ref, r_sem):
        remote(ref, ref, fy_send.at[0, 0, 0], r_sem, sibling).wait_recv()

    homes = {
        4: (far, 0), 3: (two[0], 2), 5: (two[1], 2), 2: (three[0], 6), 6: (three[1], 6),
        1: (four[0], 8), 7: (four[1], 8), 0: (last, 16),
    }

    def pick_frames(dz):
        for dy in range(NY):
            slot = send_slot[dev(z + dz, y + dy, x, c)[0]]
            if dy:
                staged[dz, dy - 1] = frames[slot]
            else:
                refs, first = homes[dz]
                for h in range(2):
                    refs[h][first + y] = frames[slot, h * HALF : (h + 1) * HALF, :]

    def send_frames(dz):
        refs, first = homes[dz]
        for h in range(2):
            for dy in (1, 3, 2):
                start(
                    staged.at[dz, dy - 1, pl.ds(h * HALF, HALF)], refs[h].at[first + y],
                    fy_send.at[dz, dy - 1, h], fy_recv.at[dz, dy - 1, h], dev(z, y + dy, x, c),
                )

    def frames_landed(dz, h):
        refs, first = homes[dz]
        for dy in (1, 3, 2):
            landed(refs[h].at[first + lax.rem(y + NY - dy, NY)], fy_recv.at[dz, dy - 1, h])

    wp[...] = jnp.zeros_like(wp)
    for t in range(NX):
        wp[t, 0:SHARD_ROWS, 0:CHUNK] = w_in[:, t * CHUNK : (t + 1) * CHUNK]
        wp[t, 0:SHARD_ROWS, CHUNK : 2 * CHUNK] = w_in[:, D + t * CHUNK : D + (t + 1) * CHUNK]
        wp[t, 0:SHARD_ROWS, 2 * CHUNK : 3 * CHUNK] = w_out[:, t * CHUNK : (t + 1) * CHUNK]
    pick_frames(4)
    pl.semaphore_wait(barrier, NX * NC + NY)

    slot_here = lax.rem(x, 2) * NC + c
    keeper = x // 2
    for t in range(NX):
        same = jnp.logical_and(x == t, keeper == c)

        @pl.when(jnp.logical_not(same))
        def _():
            remote(wp.at[t], parts.at[slot_here], part_send.at[t], part_recv.at[slot_here], (dp, t * NC + keeper)).start()

        @pl.when(same)
        def _():
            pltpu.make_async_copy(wp.at[t], parts.at[slot_here], local_sem.at[0]).start()

    send_frames(4)
    for dz in (3, 5):
        pick_frames(dz)

    for k in range(4):
        source = c * 4 + k

        @pl.when(source != fs)
        def _():
            landed(parts.at[k], part_recv.at[k])

        @pl.when(source == fs)
        def _():
            pltpu.make_async_copy(wp.at[0], parts.at[k], local_sem.at[0]).wait()

    row = lax.broadcasted_iota(jnp.int32, (BLOCK_ROWS, 32), 0)
    col = lax.broadcasted_iota(jnp.int32, (BLOCK_ROWS, 32), 1)
    pick = (col == (row // SHARD_ROWS) * 8 + lax.rem(row, SHARD_ROWS)).astype(jnp.bfloat16)
    block[...] = jnp.dot(
        pick, parts[...].reshape(32, BLOCK_COLS), preferred_element_type=jnp.float32
    ).astype(jnp.bfloat16)

    own = pltpu.make_async_copy(block, full.at[x, z, y, c], local_sem.at[1])
    own.start()

    def z_block(xx, dz, yy):
        return full.at[lax.rem(xx, NX), lax.rem(z + dz, NZ), lax.rem(yy, NY), c]

    def piece(xx, yy, half=None, cc=None):
        rows = slice(None) if half is None else pl.ds(half * 4, 4)
        return full.at[lax.rem(xx, NX), rows, lax.rem(yy, NY), c if cc is None else cc]

    def spread(i):
        dz = ARRIVALS[i]
        ref = block if i == 0 else z_block(x, dz, y)
        dst = z_block(x, dz, y)
        step = (i + 1) // 2
        if i == 0 or (dz > 4 and step < 4):
            start(ref, dst, zu_send.at[step], zu_recv.at[step], z_next[0])
        if i == 0 or (dz < 4 and step < 3):
            start(ref, dst, zd_send.at[step], zd_recv.at[step], z_next[1])
        start(ref, dst, xu_send.at[i], xu_recv.at[i], x_next[0])
        start(ref, dst, xd_send.at[i], xd_recv.at[i], x_next[1])
        start(ref, dst, yu_send.at[i], yu_recv.at[i], y_next[0])
        start(ref, dst, yd_send.at[i], yd_recv.at[i], y_next[1])

    def z_landed(i):
        dz = ARRIVALS[i]
        step = (i - 1) // 2
        recv = zu_recv if dz >= 4 else zd_recv
        landed(z_block(x, dz, y), recv.at[step])

    def hop(step, h):
        for way in range(2):
            if step == 1:
                src, dst = far[h].at[pl.ds(2 * way, 2)], two[way][h].at[pl.ds(0, 2)]
            elif step == 2:
                src, dst = two[way][h], three[way][h].at[pl.ds(0, 6)]
            elif step == 3:
                src, dst = merged3[way][h], four[way][h].at[pl.ds(0, 8)]
            else:
                src, dst = merged4[way][h], last[h].at[pl.ds(8 * way, 8)]
            start(src, dst, fz_send.at[step - 1, way, h], fz_recv.at[step - 1, way, h], z_next[way])

    def hop_landed(step, h):
        for way in range(2):
            dst = (two[way][h].at[pl.ds(0, 2)], three[way][h].at[pl.ds(0, 6)],
                   four[way][h].at[pl.ds(0, 8)], last[h].at[pl.ds(8 * way, 8)])[step - 1]
            landed(dst, fz_recv.at[step - 1, way, h])

    def merge(step, h):
        for way in range(2):
            index = (1 if step == 3 else 2) if way == 0 else (4 if step == 3 else 5)
            for r in range(RSLOT):
                source = codes[index * RSLOT + r] // 64
                zs, ys = source // NY, lax.rem(source, NY)
                away = lax.rem((z - zs if way == 0 else zs - z) + NZ, NZ)
                if step == 3:
                    early = ys - 2 * way
                    early = jnp.where(jnp.logical_and(early >= 0, early < 2), early, 0)
                    at = jnp.where(away == 0, 6 + ys, jnp.where(away == 1, 2 + ys, early))
                    merged3[way][h][r] = three[way][h][at]
                else:
                    at = jnp.where(away == 0, 8 + ys, r)
                    merged4[way][h][r] = four[way][h][at]

    def to_core(sem, ref):
        start(ref, ref, core_send.at[sem], core_recv.at[sem], sibling)

    spread(0)
    for dz in (3, 5):
        send_frames(dz)
    own.wait()
    for i in range(1, 8):
        z_landed(i)
        spread(i)
        if i == 2:
            frames_landed(4, 0)
            hop(1, 0)
        if i == 4:
            frames_landed(4, 1)
            hop(1, 1)
        if i in (5, 6):
            pick_frames((2, 6)[i - 5])
    to_core(0, piece(x, y))
    for dz in (2, 6):
        send_frames(dz)

    for h in range(2):
        hop_landed(1, h)
        frames_landed(3, h)
        frames_landed(5, h)
        hop(2, h)
    for dz in (1, 7, 0):
        pick_frames(dz)

    def x_start(j, ref):
        start(ref, ref, xu_send.at[8 + j], xu_recv.at[8 + j], x_next[0])
        start(ref, ref, xd_send.at[8 + j], xd_recv.at[8 + j], x_next[1])
        to_core(1 + j, ref)

    for i in range(8):
        landed(z_block(x, ARRIVALS[i], y + 3), yu_recv.at[i])
    ref = piece(x, y + 3, 0)
    start(ref, ref, yu_send.at[8], yu_recv.at[8], y_next[0])
    x_start(0, piece(x, y + 3))
    for i in range(8):
        landed(z_block(x, ARRIVALS[i], y + 1), yd_recv.at[i])
    ref = piece(x, y + 1, 1)
    start(ref, ref, yd_send.at[8], yd_recv.at[8], y_next[1])
    x_start(1, piece(x, y + 1))
    for dz in (1, 7, 0):
        send_frames(dz)

    for i in range(8):
        below, above = z_block(x + 3, ARRIVALS[i], y), z_block(x + 1, ARRIVALS[i], y)
        landed(below, xu_recv.at[i])
        landed(above, xd_recv.at[i])
        if i % 2 == 0:
            start(below, below, xu_send.at[12 + i // 2], xu_recv.at[12 + i // 2], x_next[0])
        else:
            start(above, above, xd_send.at[12 + i // 2], xd_recv.at[12 + i // 2], x_next[1])
    to_core(5, piece(x + 3, y))
    to_core(6, piece(x + 1, y))

    for h in range(2):
        hop_landed(2, h)
        frames_landed(2, h)
        frames_landed(6, h)
        merge(3, h)
        hop(3, h)

    landed(piece(x, y + 2, 0), yu_recv.at[8])
    x_start(2, piece(x, y + 2, 0))
    landed(piece(x, y + 2, 1), yd_recv.at[8])
    x_start(3, piece(x, y + 2, 1))

    def x_landed(j):
        dy, half = PIECES[j]
        below, above = piece(x + 3, y + dy, half), piece(x + 1, y + dy, half)
        landed(below, xu_recv.at[8 + j])
        landed(above, xd_recv.at[8 + j])
        if half in (None, 0):
            ref = piece(x + 3, y + dy, 0)
            start(ref, ref, xu_send.at[16 + j], xu_recv.at[16 + j], x_next[0])
        if half in (None, 1):
            ref = piece(x + 1, y + dy, 1)
            start(ref, ref, xd_send.at[16 + j], xd_recv.at[16 + j], x_next[1])
        to_core(7 + j, below)
        to_core(11 + j, above)

    def x_far_landed(j):
        dy, half = PIECES[j]
        if half in (None, 0):
            landed(piece(x + 2, y + dy, 0), xu_recv.at[16 + j])
        if half in (None, 1):
            landed(piece(x + 2, y + dy, 1), xd_recv.at[16 + j])
        to_core(15 + j, piece(x + 2, y + dy, half))

    x_landed(0)
    for i in range(8):
        recv = xu_recv if i % 2 == 0 else xd_recv
        landed(z_block(x + 2, ARRIVALS[i], y), recv.at[12 + i // 2])
    to_core(19, piece(x + 2, y))

    for h in range(2):
        hop_landed(3, h)
        frames_landed(1, h)
        frames_landed(7, h)
        merge(4, h)
        hop(4, h)
    x_landed(1)
    x_far_landed(0)
    x_landed(2)
    x_far_landed(1)
    x_landed(3)
    x_far_landed(2)
    x_far_landed(3)

    for h in range(2):
        hop_landed(4, h)
        frames_landed(0, h)
        for r in range(RSLOT):
            source = codes[3 * RSLOT + r] // 64
            zs, ys = source // NY, lax.rem(source, NY)
            away = lax.rem(z - zs + NZ, NZ)
            above = jnp.logical_or(away > 4, jnp.logical_and(away == 4, ys >= 2))
            at = jnp.where(away == 0, 16 + ys, jnp.where(above, 8 + r, r))
            out[r, h * HALF : (h + 1) * HALF, :] = last[h][at]

    landed(piece(x, y, None, other), core_recv.at[0])
    for j, (dy, half) in enumerate(PIECES):
        landed(piece(x, y + dy, half, other), core_recv.at[1 + j])
        landed(piece(x + 3, y + dy, half, other), core_recv.at[7 + j])
        landed(piece(x + 1, y + dy, half, other), core_recv.at[11 + j])
        landed(piece(x + 2, y + dy, half, other), core_recv.at[15 + j])
    landed(piece(x + 3, y, None, other), core_recv.at[5])
    landed(piece(x + 1, y, None, other), core_recv.at[6])
    landed(piece(x + 2, y, None, other), core_recv.at[19])

    for t in range(NX):
        same = jnp.logical_and(x == t, keeper == c)

        @pl.when(jnp.logical_not(same))
        def _():
            remote(wp.at[t], parts.at[0], part_send.at[t], part_recv.at[0], sibling).wait_send()

    for copy in started:
        copy.wait_send()


def communicate(codes, send_slot, frames, w_in, w_out):
    dma = pltpu.SemaphoreType.DMA
    smem = pl.BlockSpec(memory_space=pltpu.SMEM)
    vmem = pl.BlockSpec(memory_space=pltpu.VMEM)

    def slots(n):
        return [pltpu.VMEM((n, HALF, D), jnp.bfloat16)]

    return pl.pallas_call(
        comm_kernel,
        out_shape=(
            jax.ShapeDtypeStruct((RSLOT, MAXLEN, D), jnp.bfloat16),
            jax.ShapeDtypeStruct((NX, NZ, NY, NC, BLOCK_ROWS, BLOCK_COLS), jnp.bfloat16),
        ),
        in_specs=[smem, smem, vmem, vmem, vmem],
        out_specs=(vmem, pl.BlockSpec(memory_space=pl.ANY)),
        scratch_shapes=[
            pltpu.VMEM((NX, 8, BLOCK_COLS), jnp.bfloat16),
            pltpu.VMEM((4, 8, BLOCK_COLS), jnp.bfloat16),
            pltpu.VMEM((BLOCK_ROWS, BLOCK_COLS), jnp.bfloat16),
            pltpu.VMEM((NZ, NY - 1, MAXLEN, D), jnp.bfloat16),
            *(slots(4) * 2 + slots(6) * 4 + slots(10) * 4 + slots(12) * 4 + slots(20) * 2 + slots(8) * 8),
            dma((NZ, NY - 1, 2)), dma((NZ, NY - 1, 2)), dma((4, 2, 2)), dma((4, 2, 2)),
            dma((4,)), dma((4,)), dma((2,)),
            dma((4,)), dma((4,)), dma((3,)), dma((3,)),
            dma((9,)), dma((9,)), dma((9,)), dma((9,)),
            dma((20,)), dma((20,)), dma((20,)), dma((20,)),
            dma((20,)), dma((20,)),
        ],
        compiler_params=pltpu.CompilerParams(
            collective_id=0, has_side_effects=True, vmem_limit_bytes=40 * 1024 * 1024
        ),
        name="exchange",
    )(codes, send_slot, frames, w_in, w_out)


def module_kernel(
    codes, xbuf, full, gain, taps, scale, shift, out,
    wbuf, normed, hidden, window, act, w_sem,
):
    loads = [pltpu.make_async_copy(full.at[i], wbuf.at[i], w_sem.at[i]) for i in range(NX)]
    for load in loads:
        load.start()

    window[...] = jnp.zeros_like(window)
    def norm(r, carry):
        wide = xbuf[r].astype(jnp.float32)
        mean = jnp.mean(wide, axis=1, keepdims=True)
        centred = wide - mean
        var = jnp.mean(centred * centred, axis=1, keepdims=True)
        normed[pl.ds(pl.multiple_of(r * MAXLEN, MAXLEN), MAXLEN), :] = (
            centred * lax.rsqrt(var + 1e-05) * gain[...]
        ).astype(jnp.bfloat16)
        return carry

    lax.fori_loop(0, RSLOT, norm, 0)

    step_ids = lax.broadcasted_iota(jnp.int32, (MAXLEN, 128), 0)
    for i in range(NX):
        loads[i].wait()
        hidden[...] = jnp.dot(normed[...], wbuf[i, :, 0 : 2 * CHUNK], preferred_element_type=jnp.float32)
        for b in range(CHUNK // 128):
            lane = slice(i * CHUNK + b * 128, i * CHUNK + b * 128 + 128)
            tap = [jnp.broadcast_to(taps[k : k + 1, lane], (8, 128)) for k in range(KERNEL)]
            mul = jnp.broadcast_to(scale[:, lane], (16, 128))
            add = jnp.broadcast_to(shift[:, lane], (16, 128))

            def conv(r, carry):
                base = pl.multiple_of(r * MAXLEN, MAXLEN)
                value = hidden[pl.ds(base, MAXLEN), b * 128 : b * 128 + 128]
                gate = hidden[pl.ds(base, MAXLEN), CHUNK + b * 128 : CHUNK + b * 128 + 128]
                gated = jnp.where(step_ids < lax.rem(codes[3 * RSLOT + r], 64), value * jax.nn.sigmoid(gate), 0.0)
                window[r, PAD : PAD + MAXLEN, :] = gated
                for pair in range(2):
                    tiles = []
                    for t in (2 * pair, 2 * pair + 1):
                        total = None
                        for k in range(KERNEL):
                            first = 8 * t + k - 15
                            if first + 7 < 0 or first > MAXLEN - 1:
                                continue
                            term = window[r, PAD + first : PAD + first + 8, :] * tap[k]
                            total = term if total is None else total + term
                        tiles.append(total)
                    s = jnp.concatenate(tiles, axis=0) * mul + add
                    act[pl.ds(pl.multiple_of(base + 16 * pair, 16), 16), lane] = (
                        s * jax.nn.sigmoid(s)
                    ).astype(jnp.bfloat16)
                return carry

            lax.fori_loop(0, RSLOT, conv, 0)

    for i in range(NX):
        lane = slice(i * CHUNK, (i + 1) * CHUNK)
        hidden[:, 0:CHUNK] = jnp.dot(
            act[...], wbuf[i, :, 2 * CHUNK : 3 * CHUNK], preferred_element_type=jnp.float32
        )
        ids = lax.broadcasted_iota(jnp.int32, (MAXLEN, CHUNK), 0)

        def close(r, carry):
            mixed = xbuf[r, :, lane].astype(jnp.float32) + hidden[
                pl.ds(pl.multiple_of(r * MAXLEN, MAXLEN), MAXLEN), 0:CHUNK
            ]
            out[r, :, lane] = jnp.where(ids < lax.rem(codes[3 * RSLOT + r], 64), mixed, 0.0).astype(jnp.bfloat16)
            return carry

        lax.fori_loop(0, RSLOT, close, 0)


def conv_module(codes, xbuf, full, gain, taps, scale, shift):
    smem = pl.BlockSpec(memory_space=pltpu.SMEM)
    vmem = pl.BlockSpec(memory_space=pltpu.VMEM)
    hbm = pl.BlockSpec(memory_space=pl.ANY)
    return pl.pallas_call(
        module_kernel,
        out_shape=jax.ShapeDtypeStruct((RSLOT, MAXLEN, D), jnp.bfloat16),
        in_specs=[smem, vmem, hbm, vmem, vmem, vmem, vmem],
        out_specs=vmem,
        scratch_shapes=[
            pltpu.VMEM((NX, D, BLOCK_COLS), jnp.bfloat16),
            pltpu.VMEM((RSLOT * MAXLEN, D), jnp.bfloat16),
            pltpu.VMEM((RSLOT * MAXLEN, 2 * CHUNK), jnp.float32),
            pltpu.VMEM((RSLOT, MAXLEN + 2 * PAD, 128), jnp.float32),
            pltpu.VMEM((RSLOT * MAXLEN, D), jnp.bfloat16),
            pltpu.SemaphoreType.DMA((NX,)),
        ],
        compiler_params=pltpu.CompilerParams(vmem_limit_bytes=48 * 1024 * 1024),
        name="conv_module",
    )(codes, xbuf, full, gain, taps, scale, shift)


def shards(frames, ln_gain, w_in, depth_kernel, bn_scale, bn_shift, w_out, lengths, destinations, offsets):
    dp = lax.axis_index("dp")
    tab_len, tab_dest, tab_off = lengths[0], destinations[0], offsets[0]
    slots = tab_len.shape[1]
    peers = jnp.arange(N_DP, dtype=jnp.int32)
    own_len = lax.dynamic_index_in_dim(tab_len, dp, 0, keepdims=False)
    own_dest = lax.dynamic_index_in_dim(tab_dest, dp, 0, keepdims=False)
    sends = ((own_dest[None, :] == peers[:, None]) & (own_len[None, :] > 0)).astype(jnp.int32)
    send_slot = jnp.sum(sends * jnp.arange(slots, dtype=jnp.int32)[None, :], axis=1)

    rows = jnp.array([0, 2, 1, 0, NZ - 2, NZ - 1], dtype=jnp.int32)
    dests = lax.rem(dp // NY + rows, NZ) * NY + dp % NY
    targets = (dests[:, None] * RSLOT + jnp.arange(RSLOT, dtype=jnp.int32)[None, :]).reshape(-1)
    key = jnp.where(tab_len > 0, tab_dest * RSLOT + tab_off // MAXLEN, -1)
    code = peers[:, None] * 64 + tab_len
    codes = jnp.sum(jnp.where(key[None] == targets[:, None, None], code[None], 0), axis=(1, 2))

    xbuf, full = communicate(codes, send_slot, frames[0], w_in, w_out)
    out = conv_module(
        codes, xbuf, full.reshape(NX, D, BLOCK_COLS),
        ln_gain[None], depth_kernel, bn_scale[None], bn_shift[None],
    )
    return out[None]


def solution(mesh):
    return jax.shard_map(
        shards,
        mesh=mesh,
        in_specs=(
            P("fsdp", "dp", None, None),
            P(),
            P(("dp", "fsdp"), None),
            P(),
            P(),
            P(),
            P(("dp", "fsdp"), None),
            P("fsdp", None, None),
            P("fsdp", None, None),
            P("fsdp", None, None),
        ),
        out_specs=P("fsdp", "dp", None, None),
        check_vma=False,
    )
```

time: 184 us -> 118 us (0.64)
  Pallas kernels: 164 us -> 107 us
  other arithmetic: 6.9 us -> 2.77 us
  local copies, waits for them, and re-layouts: 11.3 us -> 7.34 us
    pallas_call x1, Pallas kernels: 147 us -> 90.6 us  [communicate(): pl.pallas_call(comm_kernel, out_shape=(jax.ShapeDtypeStruct((RSLOT, MAXLE...]
    select_n x2 -> x0, other arithmetic: 3.9 us -> none  [shards(): chosen = jnp.take(frames[0], send_slot, axis=0)]
    gather x1 -> x0, local copies, waits for them, and re-layouts: 2.38 us -> none  [shards(): chosen = jnp.take(frames[0], send_slot, axis=0)]
    unnamed x6 -> x8, local copies, waits for them, and re-layouts: 3.55 us -> 4.12 us
where the time goes in v2:
time: 118 us; the launch traced here: 117 us
  Pallas kernels  107 us (91%)
  local copies, waits for them, and re-layouts  7.34 us (6%)
  other arithmetic  2.77 us (2%)
    pallas_call x1, Pallas kernels, communicate(): pl.pallas_call(comm_kernel, out_shape=(jax.ShapeDtypeStruct((RSLOT, MAXLE...  90.6 us
    pallas_call x1, Pallas kernels, conv_module(): pl.pallas_call(module_kernel, out_shape=jax.ShapeDtypeStruct((RSLOT, MAXL...  16.5 us
    unnamed x8, local copies, waits for them, and re-layouts  4.12 us

profile of v2, /device:TPU:1, one launch (start us, length us, event | category | flops | bytes accessed | tf_op | source)
XLA Modules:
  0.0 117.2 jit_solution(15508069302619627322)
XLA Ops:
  0.0 0.7 fusion.10
  0.7 0.9 fusion.6
  1.6 0.9 dynamic-slice_reduce_fusion
  2.4 0.1 select_reduce_fusion.1.send_slot
  2.6 0.1 iota_add_fusion
  2.6 0.1 add.66
  2.7 0.7 broadcast_in_dim.40.gain
  3.4 0.7 broadcast_in_dim.41.scale
  4.1 0.7 broadcast_in_dim.42.shift
  4.8 0.8 fusion.3
  5.6 0.1 copy.16
  5.6 0.1 copy.17
  5.7 0.3 select_reduce_fusion.codes
  6.0 0.0 copy-start
  6.0 1.7 %copy-done = bf16[1,24,32,1536]{3,2,1,0:T(8,128)(2,1)S(1)} copy-done((bf16[1,24,32,1536]{3,2,1,0:T(8,128)(2,1)S(1)}, bf16[1,24,32,1536]{3,2,1,0:T(8,128)(2,1)}, u32[]{:S(2)}) %copy-start) | copy-done | bytes 2359320
  7.7 0.0 copy-start.2
  7.7 0.8 copy-done.2
  8.5 0.0 copy-start.3
  8.5 0.7 copy-done.3
  9.2 90.6 %exchange.1 = (bf16[8,32,1536]{2,1,0:T(8,128)(2,1)S(1)}, bf16[4,8,4,2,24,1152]{5,4,3,2,1,0:T(8,128)(2,1)}) custom-call(s32[48]{0:T(128)S(1)} %select_reduce_fusion.codes, s32[32]{0:T(128)S(1)} %select_reduce_fusion.1.send_slot, bf16[24,32,1536]{2,1,0:T(8,128)(2,1)S(1)} %bitcast.7, bf16[6,3072]{1,0:T(8,128)(2,1)S(1)} %copy-done.2, bf16[6,1536]{1,0:T(8,128)(2,1)S(1)} %copy-done.3), custom_call_target="tpu_custom_call" | custom-call | tf_op jit(solution)/shard_map/exchange/pallas_call | solution.py:376
  99.8 0.0 copy-start.1
  99.8 0.9 copy-done.1
  100.7 16.5 %conv_module.1 = bf16[8,32,1536]{2,1,0:T(8,128)(2,1)} custom-call(s32[48]{0:T(128)S(1)} %select_reduce_fusion.codes, bf16[8,32,1536]{2,1,0:T(8,128)(2,1)S(1)} %get-tuple-element.7.xbuf, bf16[4,1536,1152]{2,1,0:T(8,128)(2,1)} %bitcast.8, f32[1,1536]{1,0:T(1,128)S(1)} %broadcast_in_dim.40.gain, f32[31,1536]{1,0:T(8,128)S(1)} %copy-done.1, ...), custom_call_target="tpu_custom_call" | custom-call | tf_op jit(solution)/shard_map/conv_module/pallas_call | solution.py:481
  (1 shorter events, 0.0 us)
Async XLA Ops:
  6.0 1.7 %copy-start = (bf16[1,24,32,1536]{3,2,1,0:T(8,128)(2,1)S(1)}, bf16[1,24,32,1536]{3,2,1,0:T(8,128)(2,1)}, u32[]{:S(2)}) copy-start(bf16[1,24,32,1536]{3,2,1,0:T(8,128)(2,1)} %param.11) | copy-start | bytes 7077892
  7.7 0.8 copy-start.2
  8.5 0.7 copy-start.3
  99.8 0.9 copy-start.1

commit v3 on v2

--- a/solution.py
+++ b/solution.py
@@ -26,8 +26,8 @@
 
 
 def comm_kernel(
-    codes, send_slot, frames, w_in, w_out, out, full,
-    wp, parts, block, staged,
+    codes, frames_hbm, w_in_hbm, w_out_hbm, out, full,
+    frames, w_in, w_out, wp, parts, block, staged,
     far0, far1, up2_0, up2_1, dn2_0, dn2_1, up3_0, up3_1, dn3_0, dn3_1, up4_0, up4_1, dn4_0, dn4_1, last0, last1,
     mu3_0, mu3_1, md3_0, md3_1, mu4_0, mu4_1, md4_0, md4_1,
     fy_send, fy_recv, fz_send, fz_recv,
@@ -69,6 +69,14 @@
     for device in z_next:
         greet(device)
 
+    loads = [
+        pltpu.make_async_copy(w_in_hbm, w_in, local_sem.at[2]),
+        pltpu.make_async_copy(w_out_hbm, w_out, local_sem.at[3]),
+        pltpu.make_async_copy(frames_hbm, frames, local_sem.at[4]),
+    ]
+    for load in loads:
+        load.start()
+
     def remote(src, dst, send, recv, device):
         return pltpu.make_async_remote_copy(
             src_ref=src, dst_ref=dst, send_sem=send, recv_sem=recv, device_id=device, device_id_type=MESH
@@ -91,7 +99,7 @@
 
     def pick_frames(dz):
         for dy in range(NY):
-            slot = send_slot[dev(z + dz, y + dy, x, c)[0]]
+            slot = codes[6 * RSLOT + dev(z + dz, y + dy, x, c)[0]]
             if dy:
                 staged[dz, dy - 1] = frames[slot]
             else:
@@ -114,10 +122,13 @@
             landed(refs[h].at[first + lax.rem(y + NY - dy, NY)], fy_recv.at[dz, dy - 1, h])
 
     wp[...] = jnp.zeros_like(wp)
+    for load in loads[:2]:
+        load.wait()
     for t in range(NX):
         wp[t, 0:SHARD_ROWS, 0:CHUNK] = w_in[:, t * CHUNK : (t + 1) * CHUNK]
         wp[t, 0:SHARD_ROWS, CHUNK : 2 * CHUNK] = w_in[:, D + t * CHUNK : D + (t + 1) * CHUNK]
         wp[t, 0:SHARD_ROWS, 2 * CHUNK : 3 * CHUNK] = w_out[:, t * CHUNK : (t + 1) * CHUNK]
+    loads[2].wait()
     pick_frames(4)
     pl.semaphore_wait(barrier, NX * NC + NY)
 
@@ -365,10 +376,11 @@
         copy.wait_send()
 
 
-def communicate(codes, send_slot, frames, w_in, w_out):
+def communicate(codes, frames, w_in, w_out):
     dma = pltpu.SemaphoreType.DMA
     smem = pl.BlockSpec(memory_space=pltpu.SMEM)
     vmem = pl.BlockSpec(memory_space=pltpu.VMEM)
+    hbm = pl.BlockSpec(memory_space=pltpu.HBM)
 
     def slots(n):
         return [pltpu.VMEM((n, HALF, D), jnp.bfloat16)]
@@ -379,26 +391,29 @@
             jax.ShapeDtypeStruct((RSLOT, MAXLEN, D), jnp.bfloat16),
             jax.ShapeDtypeStruct((NX, NZ, NY, NC, BLOCK_ROWS, BLOCK_COLS), jnp.bfloat16),
         ),
-        in_specs=[smem, smem, vmem, vmem, vmem],
+        in_specs=[smem, hbm, hbm, hbm],
         out_specs=(vmem, pl.BlockSpec(memory_space=pl.ANY)),
         scratch_shapes=[
+            pltpu.VMEM(frames.shape, jnp.bfloat16),
+            pltpu.VMEM(w_in.shape, jnp.bfloat16),
+            pltpu.VMEM(w_out.shape, jnp.bfloat16),
             pltpu.VMEM((NX, 8, BLOCK_COLS), jnp.bfloat16),
             pltpu.VMEM((4, 8, BLOCK_COLS), jnp.bfloat16),
             pltpu.VMEM((BLOCK_ROWS, BLOCK_COLS), jnp.bfloat16),
             pltpu.VMEM((NZ, NY - 1, MAXLEN, D), jnp.bfloat16),
             *(slots(4) * 2 + slots(6) * 4 + slots(10) * 4 + slots(12) * 4 + slots(20) * 2 + slots(8) * 8),
             dma((NZ, NY - 1, 2)), dma((NZ, NY - 1, 2)), dma((4, 2, 2)), dma((4, 2, 2)),
-            dma((4,)), dma((4,)), dma((2,)),
+            dma((4,)), dma((4,)), dma((5,)),
             dma((4,)), dma((4,)), dma((3,)), dma((3,)),
             dma((9,)), dma((9,)), dma((9,)), dma((9,)),
             dma((20,)), dma((20,)), dma((20,)), dma((20,)),
             dma((20,)), dma((20,)),
         ],
         compiler_params=pltpu.CompilerParams(
-            collective_id=0, has_side_effects=True, vmem_limit_bytes=40 * 1024 * 1024
+            collective_id=0, has_side_effects=True, vmem_limit_bytes=67043328
         ),
         name="exchange",
-    )(codes, send_slot, frames, w_in, w_out)
+    )(codes, frames, w_in, w_out)
 
 
 def module_kernel(
@@ -410,14 +425,15 @@
         load.start()
 
     window[...] = jnp.zeros_like(window)
-    def norm(r, carry):
-        wide = xbuf[r].astype(jnp.float32)
-        mean = jnp.mean(wide, axis=1, keepdims=True)
-        centred = wide - mean
-        var = jnp.mean(centred * centred, axis=1, keepdims=True)
-        normed[pl.ds(pl.multiple_of(r * MAXLEN, MAXLEN), MAXLEN), :] = (
-            centred * lax.rsqrt(var + 1e-05) * gain[...]
-        ).astype(jnp.bfloat16)
+    def norm(i, carry):
+        for h in range(2):
+            wide = xbuf[i, h * HALF : (h + 1) * HALF, :].astype(jnp.float32)
+            mean = jnp.mean(wide, axis=1, keepdims=True)
+            centred = wide - mean
+            var = jnp.mean(centred * centred, axis=1, keepdims=True)
+            normed[pl.ds(pl.multiple_of(i * MAXLEN + h * HALF, HALF), HALF), :] = (
+                centred * lax.rsqrt(var + 1e-05) * gain[...].reshape(1, D)
+            ).astype(jnp.bfloat16)
         return carry
 
     lax.fori_loop(0, RSLOT, norm, 0)
@@ -429,8 +445,8 @@
         for b in range(CHUNK // 128):
             lane = slice(i * CHUNK + b * 128, i * CHUNK + b * 128 + 128)
             tap = [jnp.broadcast_to(taps[k : k + 1, lane], (8, 128)) for k in range(KERNEL)]
-            mul = jnp.broadcast_to(scale[:, lane], (16, 128))
-            add = jnp.broadcast_to(shift[:, lane], (16, 128))
+            mul = jnp.broadcast_to(scale[lane].reshape(1, 128), (16, 128))
+            add = jnp.broadcast_to(shift[lane].reshape(1, 128), (16, 128))
 
             def conv(r, carry):
                 base = pl.multiple_of(r * MAXLEN, MAXLEN)
@@ -438,24 +454,22 @@
                 gate = hidden[pl.ds(base, MAXLEN), CHUNK + b * 128 : CHUNK + b * 128 + 128]
                 gated = jnp.where(step_ids < lax.rem(codes[3 * RSLOT + r], 64), value * jax.nn.sigmoid(gate), 0.0)
                 window[r, PAD : PAD + MAXLEN, :] = gated
+                total = [None] * 4
+                for first in range(-7, MAXLEN):
+                    rows = window[r, PAD + first : PAD + first + 8, :]
+                    for t in range(4):
+                        k = first + 15 - 8 * t
+                        if 0 <= k < KERNEL:
+                            term = rows * tap[k]
+                            total[t] = term if total[t] is None else total[t] + term
                 for pair in range(2):
-                    tiles = []
-                    for t in (2 * pair, 2 * pair + 1):
-                        total = None
-                        for k in range(KERNEL):
-                            first = 8 * t + k - 15
-                            if first + 7 < 0 or first > MAXLEN - 1:
-                                continue
-                            term = window[r, PAD + first : PAD + first + 8, :] * tap[k]
-                            total = term if total is None else total + term
-                        tiles.append(total)
-                    s = jnp.concatenate(tiles, axis=0) * mul + add
+                    s = jnp.concatenate(total[2 * pair : 2 * pair + 2], axis=0) * mul + add
                     act[pl.ds(pl.multiple_of(base + 16 * pair, 16), 16), lane] = (
                         s * jax.nn.sigmoid(s)
                     ).astype(jnp.bfloat16)
                 return carry
 
-            lax.fori_loop(0, RSLOT, conv, 0)
+            lax.fori_loop(0, RSLOT, conv, 0, unroll=4)
 
     for i in range(NX):
         lane = slice(i * CHUNK, (i + 1) * CHUNK)
@@ -477,7 +491,7 @@
 def conv_module(codes, xbuf, full, gain, taps, scale, shift):
     smem = pl.BlockSpec(memory_space=pltpu.SMEM)
     vmem = pl.BlockSpec(memory_space=pltpu.VMEM)
-    hbm = pl.BlockSpec(memory_space=pl.ANY)
+    hbm = pl.BlockSpec(memory_space=pltpu.HBM)
     return pl.pallas_call(
         module_kernel,
         out_shape=jax.ShapeDtypeStruct((RSLOT, MAXLEN, D), jnp.bfloat16),
@@ -491,7 +505,7 @@
             pltpu.VMEM((RSLOT * MAXLEN, D), jnp.bfloat16),
             pltpu.SemaphoreType.DMA((NX,)),
         ],
-        compiler_params=pltpu.CompilerParams(vmem_limit_bytes=48 * 1024 * 1024),
+        compiler_params=pltpu.CompilerParams(vmem_limit_bytes=67043328),
         name="conv_module",
     )(codes, xbuf, full, gain, taps, scale, shift)
 
@@ -501,22 +515,25 @@
     tab_len, tab_dest, tab_off = lengths[0], destinations[0], offsets[0]
     slots = tab_len.shape[1]
     peers = jnp.arange(N_DP, dtype=jnp.int32)
-    own_len = lax.dynamic_index_in_dim(tab_len, dp, 0, keepdims=False)
-    own_dest = lax.dynamic_index_in_dim(tab_dest, dp, 0, keepdims=False)
-    sends = ((own_dest[None, :] == peers[:, None]) & (own_len[None, :] > 0)).astype(jnp.int32)
-    send_slot = jnp.sum(sends * jnp.arange(slots, dtype=jnp.int32)[None, :], axis=1)
-
-    rows = jnp.array([0, 2, 1, 0, NZ - 2, NZ - 1], dtype=jnp.int32)
-    dests = lax.rem(dp // NY + rows, NZ) * NY + dp % NY
-    targets = (dests[:, None] * RSLOT + jnp.arange(RSLOT, dtype=jnp.int32)[None, :]).reshape(-1)
-    key = jnp.where(tab_len > 0, tab_dest * RSLOT + tab_off // MAXLEN, -1)
-    code = peers[:, None] * 64 + tab_len
-    codes = jnp.sum(jnp.where(key[None] == targets[:, None, None], code[None], 0), axis=(1, 2))
-
-    xbuf, full = communicate(codes, send_slot, frames[0], w_in, w_out)
+    entry = jnp.arange(6 * RSLOT + N_DP, dtype=jnp.int32)
+    ahead = jnp.array([0, 2, 1, 0, NZ - 2, NZ - 1] + [0] * 4, dtype=jnp.int32)[:, None] * jnp.ones((1, RSLOT), jnp.int32)
+    dests = lax.rem(dp // NY + ahead.reshape(-1), NZ) * NY + dp % NY
+    incoming = entry < 6 * RSLOT
+    targets = jnp.where(incoming, dests * RSLOT + entry % RSLOT, entry - 6 * RSLOT)[:, None, None]
+    incoming = incoming[:, None, None]
+    live = tab_len > 0
+    key_in = jnp.where(live, tab_dest * RSLOT + tab_off // MAXLEN, -1)
+    key_out = jnp.where(live & (peers[:, None] == dp), tab_dest, -1)
+    code_in = peers[:, None] * 64 + tab_len
+    code_out = jnp.broadcast_to(jnp.arange(slots, dtype=jnp.int32)[None, :], tab_len.shape)
+    key = jnp.where(incoming, key_in[None], key_out[None])
+    value = jnp.where(incoming, code_in[None], code_out[None])
+    codes = jnp.sum(jnp.where(key == targets, value, 0), axis=(1, 2))
+
+    xbuf, full = communicate(codes, frames[0], w_in, w_out)
     out = conv_module(
         codes, xbuf, full.reshape(NX, D, BLOCK_COLS),
-        ln_gain[None], depth_kernel, bn_scale[None], bn_shift[None],
+        ln_gain, depth_kernel, bn_scale, bn_shift,
     )
     return out[None]
 

time: 118 us -> 110 us (0.932)
  local copies, waits for them, and re-layouts: 7.34 us -> 0.37 us
    unnamed x8 -> x0, local copies, waits for them, and re-layouts: 4.12 us -> none
    broadcast_in_dim x4 -> x3, local copies, waits for them, and re-layouts: 2.18 us -> 0.22 us  [the longest x2 0.15 us: shards(): key = jnp.where(incoming, key_in[None], key_out[None])]
    pallas_call x1, Pallas kernels: 16.5 us -> 14.7 us  [conv_module(): pl.pallas_call(module_kernel, out_shape=jax.ShapeDtypeStruct((RSLOT, MAXL...]
    broadcast_in_dim x0 -> x2, other arithmetic: none -> 1.48 us  [shards(): key = jnp.where(incoming, key_in[None], key_out[None])]
where the time goes in v3:
time: 110 us
  Pallas kernels  106 us (96%)
  other arithmetic  3.22 us (3%)
    pallas_call x1, Pallas kernels, communicate(): pl.pallas_call(comm_kernel, out_shape=(jax.ShapeDtypeStruct((RSLOT, MAXLE...  91.6 us
    pallas_call x1, Pallas kernels, conv_module(): pl.pallas_call(module_kernel, out_shape=jax.ShapeDtypeStruct((RSLOT, MAXL...  14.7 us

profile of v3, /device:TPU:1, one launch (start us, length us, event | category | flops | bytes accessed | tf_op | source)
XLA Modules:
  0.0 109.9 jit_solution(1928772077200107564)
XLA Ops:
  0.0 0.7 broadcast_add_fusion
  0.7 0.1 mul.42
  0.7 0.1 add.69
  0.8 0.8 fusion.3
  1.6 0.1 copy.18
  1.7 0.7 select_bitcast_fusion
  2.4 0.1 copy.19
  2.5 0.1 copy.20
  2.5 1.1 select_reduce_fusion.codes
  3.6 91.6 %exchange.1 = (bf16[8,32,1536]{2,1,0:T(8,128)(2,1)}, bf16[4,8,4,2,24,1152]{5,4,3,2,1,0:T(8,128)(2,1)}) custom-call(s32[80]{0:T(128)} %select_reduce_fusion.codes, bf16[24,32,1536]{2,1,0:T(8,128)(2,1)} %bitcast.10, bf16[6,3072]{1,0:T(8,128)(2,1)} %w_in_hbm.1, bf16[6,1536]{1,0:T(8,128)(2,1)} %w_out_hbm.1), custom_call_target="tpu_custom_call" | custom-call | tf_op jit(solution)/shard_map/exchange/pallas_call | solution.py:388
  95.2 14.7 %conv_module.1 = bf16[8,32,1536]{2,1,0:T(8,128)(2,1)} custom-call(s32[80]{0:T(128)} %select_reduce_fusion.codes, bf16[8,32,1536]{2,1,0:T(8,128)(2,1)} %get-tuple-element.7.xbuf, bf16[4,1536,1152]{2,1,0:T(8,128)(2,1)} %bitcast.9, f32[1536]{0:T(1024)} %gain.1, f32[31,1536]{1,0:T(8,128)} %taps.1, f32[1536]{0:T(1024)} %scale.1, f32[1536]{0:T(1024)} %shift.1), custom_call_target="tpu_custom_call" | custom-call | tf_op jit(solution)/shard_map/conv_module/pallas_call | solution.py:495
  (4 shorter events, 0.0 us)

commit v4 on v3

--- a/solution.py
+++ b/solution.py
@@ -22,11 +22,12 @@
 HALF = MAXLEN // 2
 PIECES = [(3, None), (1, None), (2, 0), (2, 1)]
 ARRIVALS = [0, 7, 1, 6, 2, 5, 3, 4]
-UP_FORWARD = (0, 1, 2, 3)
+ORDER = (0, 3, 1, 2)
 
 
 def comm_kernel(
-    codes, frames_hbm, w_in_hbm, w_out_hbm, out, full,
+    codes, frames_hbm, w_in_hbm, w_out_hbm, gain_hbm, taps_hbm, scale_hbm, shift_hbm, out, full,
+    xbuf, wbuf, normed, hidden, window, act, gain, taps, scale, shift, w_sem,
     frames, w_in, w_out, wp, parts, block, staged,
     far0, far1, up2_0, up2_1, dn2_0, dn2_1, up3_0, up3_1, dn3_0, dn3_1, up4_0, up4_1, dn4_0, dn4_1, last0, last1,
     mu3_0, mu3_1, md3_0, md3_1, mu4_0, mu4_1, md4_0, md4_1,
@@ -49,6 +50,9 @@
     merged3 = ((mu3_0, mu3_1), (md3_0, md3_1))
     merged4 = ((mu4_0, mu4_1), (md4_0, md4_1))
 
+    def kept(cc):
+        return pl.ds(pl.multiple_of(cc * BLOCK_ROWS, 8), BLOCK_ROWS)
+
     def dev(zz, yy, xx, cc):
         return (lax.rem(zz, NZ) * NY + lax.rem(yy, NY), lax.rem(xx, NX) * NC + cc)
 
@@ -73,6 +77,10 @@
         pltpu.make_async_copy(w_in_hbm, w_in, local_sem.at[2]),
         pltpu.make_async_copy(w_out_hbm, w_out, local_sem.at[3]),
         pltpu.make_async_copy(frames_hbm, frames, local_sem.at[4]),
+        pltpu.make_async_copy(gain_hbm, gain, local_sem.at[5]),
+        pltpu.make_async_copy(taps_hbm, taps, local_sem.at[6]),
+        pltpu.make_async_copy(scale_hbm, scale, local_sem.at[7]),
+        pltpu.make_async_copy(shift_hbm, shift, local_sem.at[8]),
     ]
     for load in loads:
         load.start()
@@ -122,6 +130,7 @@
             landed(refs[h].at[first + lax.rem(y + NY - dy, NY)], fy_recv.at[dz, dy - 1, h])
 
     wp[...] = jnp.zeros_like(wp)
+    window[...] = jnp.zeros_like(window)
     for load in loads[:2]:
         load.wait()
     for t in range(NX):
@@ -167,15 +176,15 @@
         pick, parts[...].reshape(32, BLOCK_COLS), preferred_element_type=jnp.float32
     ).astype(jnp.bfloat16)
 
-    own = pltpu.make_async_copy(block, full.at[x, z, y, c], local_sem.at[1])
+    own = pltpu.make_async_copy(block, full.at[x, z, y, kept(c)], local_sem.at[1])
     own.start()
 
     def z_block(xx, dz, yy):
-        return full.at[lax.rem(xx, NX), lax.rem(z + dz, NZ), lax.rem(yy, NY), c]
+        return full.at[lax.rem(xx, NX), lax.rem(z + dz, NZ), lax.rem(yy, NY), kept(c)]
 
     def piece(xx, yy, half=None, cc=None):
         rows = slice(None) if half is None else pl.ds(half * 4, 4)
-        return full.at[lax.rem(xx, NX), rows, lax.rem(yy, NY), c if cc is None else cc]
+        return full.at[lax.rem(xx, NX), rows, lax.rem(yy, NY), kept(c if cc is None else cc)]
 
     def spread(i):
         dz = ARRIVALS[i]
@@ -234,197 +243,8 @@
     def to_core(sem, ref):
         start(ref, ref, core_send.at[sem], core_recv.at[sem], sibling)
 
-    spread(0)
-    for dz in (3, 5):
-        send_frames(dz)
-    own.wait()
-    for i in range(1, 8):
-        z_landed(i)
-        spread(i)
-        if i == 2:
-            frames_landed(4, 0)
-            hop(1, 0)
-        if i == 4:
-            frames_landed(4, 1)
-            hop(1, 1)
-        if i in (5, 6):
-            pick_frames((2, 6)[i - 5])
-    to_core(0, piece(x, y))
-    for dz in (2, 6):
-        send_frames(dz)
-
-    for h in range(2):
-        hop_landed(1, h)
-        frames_landed(3, h)
-        frames_landed(5, h)
-        hop(2, h)
-    for dz in (1, 7, 0):
-        pick_frames(dz)
-
-    def x_start(j, ref):
-        start(ref, ref, xu_send.at[8 + j], xu_recv.at[8 + j], x_next[0])
-        start(ref, ref, xd_send.at[8 + j], xd_recv.at[8 + j], x_next[1])
-        to_core(1 + j, ref)
-
-    for i in range(8):
-        landed(z_block(x, ARRIVALS[i], y + 3), yu_recv.at[i])
-    ref = piece(x, y + 3, 0)
-    start(ref, ref, yu_send.at[8], yu_recv.at[8], y_next[0])
-    x_start(0, piece(x, y + 3))
-    for i in range(8):
-        landed(z_block(x, ARRIVALS[i], y + 1), yd_recv.at[i])
-    ref = piece(x, y + 1, 1)
-    start(ref, ref, yd_send.at[8], yd_recv.at[8], y_next[1])
-    x_start(1, piece(x, y + 1))
-    for dz in (1, 7, 0):
-        send_frames(dz)
-
-    for i in range(8):
-        below, above = z_block(x + 3, ARRIVALS[i], y), z_block(x + 1, ARRIVALS[i], y)
-        landed(below, xu_recv.at[i])
-        landed(above, xd_recv.at[i])
-        if i % 2 == 0:
-            start(below, below, xu_send.at[12 + i // 2], xu_recv.at[12 + i // 2], x_next[0])
-        else:
-            start(above, above, xd_send.at[12 + i // 2], xd_recv.at[12 + i // 2], x_next[1])
-    to_core(5, piece(x + 3, y))
-    to_core(6, piece(x + 1, y))
-
-    for h in range(2):
-        hop_landed(2, h)
-        frames_landed(2, h)
-        frames_landed(6, h)
-        merge(3, h)
-        hop(3, h)
-
-    landed(piece(x, y + 2, 0), yu_recv.at[8])
-    x_start(2, piece(x, y + 2, 0))
-    landed(piece(x, y + 2, 1), yd_recv.at[8])
-    x_start(3, piece(x, y + 2, 1))
-
-    def x_landed(j):
-        dy, half = PIECES[j]
-        below, above = piece(x + 3, y + dy, half), piece(x + 1, y + dy, half)
-        landed(below, xu_recv.at[8 + j])
-        landed(above, xd_recv.at[8 + j])
-        if half in (None, 0):
-            ref = piece(x + 3, y + dy, 0)
-            start(ref, ref, xu_send.at[16 + j], xu_recv.at[16 + j], x_next[0])
-        if half in (None, 1):
-            ref = piece(x + 1, y + dy, 1)
-            start(ref, ref, xd_send.at[16 + j], xd_recv.at[16 + j], x_next[1])
-        to_core(7 + j, below)
-        to_core(11 + j, above)
-
-    def x_far_landed(j):
-        dy, half = PIECES[j]
-        if half in (None, 0):
-            landed(piece(x + 2, y + dy, 0), xu_recv.at[16 + j])
-        if half in (None, 1):
-            landed(piece(x + 2, y + dy, 1), xd_recv.at[16 + j])
-        to_core(15 + j, piece(x + 2, y + dy, half))
-
-    x_landed(0)
-    for i in range(8):
-        recv = xu_recv if i % 2 == 0 else xd_recv
-        landed(z_block(x + 2, ARRIVALS[i], y), recv.at[12 + i // 2])
-    to_core(19, piece(x + 2, y))
-
-    for h in range(2):
-        hop_landed(3, h)
-        frames_landed(1, h)
-        frames_landed(7, h)
-        merge(4, h)
-        hop(4, h)
-    x_landed(1)
-    x_far_landed(0)
-    x_landed(2)
-    x_far_landed(1)
-    x_landed(3)
-    x_far_landed(2)
-    x_far_landed(3)
-
-    for h in range(2):
-        hop_landed(4, h)
-        frames_landed(0, h)
-        for r in range(RSLOT):
-            source = codes[3 * RSLOT + r] // 64
-            zs, ys = source // NY, lax.rem(source, NY)
-            away = lax.rem(z - zs + NZ, NZ)
-            above = jnp.logical_or(away > 4, jnp.logical_and(away == 4, ys >= 2))
-            at = jnp.where(away == 0, 16 + ys, jnp.where(above, 8 + r, r))
-            out[r, h * HALF : (h + 1) * HALF, :] = last[h][at]
-
-    landed(piece(x, y, None, other), core_recv.at[0])
-    for j, (dy, half) in enumerate(PIECES):
-        landed(piece(x, y + dy, half, other), core_recv.at[1 + j])
-        landed(piece(x + 3, y + dy, half, other), core_recv.at[7 + j])
-        landed(piece(x + 1, y + dy, half, other), core_recv.at[11 + j])
-        landed(piece(x + 2, y + dy, half, other), core_recv.at[15 + j])
-    landed(piece(x + 3, y, None, other), core_recv.at[5])
-    landed(piece(x + 1, y, None, other), core_recv.at[6])
-    landed(piece(x + 2, y, None, other), core_recv.at[19])
-
-    for t in range(NX):
-        same = jnp.logical_and(x == t, keeper == c)
-
-        @pl.when(jnp.logical_not(same))
-        def _():
-            remote(wp.at[t], parts.at[0], part_send.at[t], part_recv.at[0], sibling).wait_send()
-
-    for copy in started:
-        copy.wait_send()
-
-
-def communicate(codes, frames, w_in, w_out):
-    dma = pltpu.SemaphoreType.DMA
-    smem = pl.BlockSpec(memory_space=pltpu.SMEM)
-    vmem = pl.BlockSpec(memory_space=pltpu.VMEM)
-    hbm = pl.BlockSpec(memory_space=pltpu.HBM)
-
-    def slots(n):
-        return [pltpu.VMEM((n, HALF, D), jnp.bfloat16)]
-
-    return pl.pallas_call(
-        comm_kernel,
-        out_shape=(
-            jax.ShapeDtypeStruct((RSLOT, MAXLEN, D), jnp.bfloat16),
-            jax.ShapeDtypeStruct((NX, NZ, NY, NC, BLOCK_ROWS, BLOCK_COLS), jnp.bfloat16),
-        ),
-        in_specs=[smem, hbm, hbm, hbm],
-        out_specs=(vmem, pl.BlockSpec(memory_space=pl.ANY)),
-        scratch_shapes=[
-            pltpu.VMEM(frames.shape, jnp.bfloat16),
-            pltpu.VMEM(w_in.shape, jnp.bfloat16),
-            pltpu.VMEM(w_out.shape, jnp.bfloat16),
-            pltpu.VMEM((NX, 8, BLOCK_COLS), jnp.bfloat16),
-            pltpu.VMEM((4, 8, BLOCK_COLS), jnp.bfloat16),
-            pltpu.VMEM((BLOCK_ROWS, BLOCK_COLS), jnp.bfloat16),
-            pltpu.VMEM((NZ, NY - 1, MAXLEN, D), jnp.bfloat16),
-            *(slots(4) * 2 + slots(6) * 4 + slots(10) * 4 + slots(12) * 4 + slots(20) * 2 + slots(8) * 8),
-            dma((NZ, NY - 1, 2)), dma((NZ, NY - 1, 2)), dma((4, 2, 2)), dma((4, 2, 2)),
-            dma((4,)), dma((4,)), dma((5,)),
-            dma((4,)), dma((4,)), dma((3,)), dma((3,)),
-            dma((9,)), dma((9,)), dma((9,)), dma((9,)),
-            dma((20,)), dma((20,)), dma((20,)), dma((20,)),
-            dma((20,)), dma((20,)),
-        ],
-        compiler_params=pltpu.CompilerParams(
-            collective_id=0, has_side_effects=True, vmem_limit_bytes=67043328
-        ),
-        name="exchange",
-    )(codes, frames, w_in, w_out)
-
-
-def module_kernel(
-    codes, xbuf, full, gain, taps, scale, shift, out,
-    wbuf, normed, hidden, window, act, w_sem,
-):
-    loads = [pltpu.make_async_copy(full.at[i], wbuf.at[i], w_sem.at[i]) for i in range(NX)]
-    for load in loads:
-        load.start()
-
-    window[...] = jnp.zeros_like(window)
+    step_ids = lax.broadcasted_iota(jnp.int32, (MAXLEN, 128), 0)
+
     def norm(i, carry):
         for h in range(2):
             wide = xbuf[i, h * HALF : (h + 1) * HALF, :].astype(jnp.float32)
@@ -436,14 +256,17 @@
             ).astype(jnp.bfloat16)
         return carry
 
-    lax.fori_loop(0, RSLOT, norm, 0)
-
-    step_ids = lax.broadcasted_iota(jnp.int32, (MAXLEN, 128), 0)
-    for i in range(NX):
-        loads[i].wait()
-        hidden[...] = jnp.dot(normed[...], wbuf[i, :, 0 : 2 * CHUNK], preferred_element_type=jnp.float32)
+    def load_chunk(i):
+        return pltpu.make_async_copy(
+            full.at[lax.rem(x + ORDER[i], NX)], wbuf.at[i], w_sem.at[i]
+        )
+
+    def chunk(i):
+        column = lax.rem(x + ORDER[i], NX) * CHUNK
+        load_chunk(i).wait()
+        hidden[...] = jnp.dot(normed[...], wbuf[i, :, :, :, 0 : 2 * CHUNK].reshape(D, 2 * CHUNK), preferred_element_type=jnp.float32)
         for b in range(CHUNK // 128):
-            lane = slice(i * CHUNK + b * 128, i * CHUNK + b * 128 + 128)
+            lane = pl.ds(pl.multiple_of(column + b * 128, 128), 128)
             tap = [jnp.broadcast_to(taps[k : k + 1, lane], (8, 128)) for k in range(KERNEL)]
             mul = jnp.broadcast_to(scale[lane].reshape(1, 128), (16, 128))
             add = jnp.broadcast_to(shift[lane].reshape(1, 128), (16, 128))
@@ -471,11 +294,153 @@
 
             lax.fori_loop(0, RSLOT, conv, 0, unroll=4)
 
+    spread(0)
+    for dz in (3, 5):
+        send_frames(dz)
+    own.wait()
+    for i in range(1, 8):
+        z_landed(i)
+        spread(i)
+        if i == 2:
+            frames_landed(4, 0)
+            hop(1, 0)
+        if i == 4:
+            frames_landed(4, 1)
+            hop(1, 1)
+        if i in (5, 6):
+            pick_frames((2, 6)[i - 5])
+    to_core(0, piece(x, y))
+    for dz in (2, 6):
+        send_frames(dz)
+
+    for h in range(2):
+        hop_landed(1, h)
+        frames_landed(3, h)
+        frames_landed(5, h)
+        hop(2, h)
+    for dz in (1, 7, 0):
+        pick_frames(dz)
+
+    def x_start(j, ref):
+        start(ref, ref, xu_send.at[8 + j], xu_recv.at[8 + j], x_next[0])
+        start(ref, ref, xd_send.at[8 + j], xd_recv.at[8 + j], x_next[1])
+        to_core(1 + j, ref)
+
+    for i in range(8):
+        landed(z_block(x, ARRIVALS[i], y + 3), yu_recv.at[i])
+    ref = piece(x, y + 3, 0)
+    start(ref, ref, yu_send.at[8], yu_recv.at[8], y_next[0])
+    x_start(0, piece(x, y + 3))
+    for i in range(8):
+        landed(z_block(x, ARRIVALS[i], y + 1), yd_recv.at[i])
+    ref = piece(x, y + 1, 1)
+    start(ref, ref, yd_send.at[8], yd_recv.at[8], y_next[1])
+    x_start(1, piece(x, y + 1))
+    for dz in (1, 7, 0):
+        send_frames(dz)
+
+    for i in range(8):
+        below, above = z_block(x + 3, ARRIVALS[i], y), z_block(x + 1, ARRIVALS[i], y)
+        landed(below, xu_recv.at[i])
+        landed(above, xd_recv.at[i])
+        if i % 2 == 0:
+            start(below, below, xu_send.at[12 + i // 2], xu_recv.at[12 + i // 2], x_next[0])
+        else:
+            start(above, above, xd_send.at[12 + i // 2], xd_recv.at[12 + i // 2], x_next[1])
+    to_core(5, piece(x + 3, y))
+    to_core(6, piece(x + 1, y))
+
+    for h in range(2):
+        hop_landed(2, h)
+        frames_landed(2, h)
+        frames_landed(6, h)
+        merge(3, h)
+        hop(3, h)
+
+    landed(piece(x, y + 2, 0), yu_recv.at[8])
+    x_start(2, piece(x, y + 2, 0))
+    landed(piece(x, y + 2, 1), yd_recv.at[8])
+    x_start(3, piece(x, y + 2, 1))
+
+    def x_landed(j):
+        dy, half = PIECES[j]
+        below, above = piece(x + 3, y + dy, half), piece(x + 1, y + dy, half)
+        landed(below, xu_recv.at[8 + j])
+        landed(above, xd_recv.at[8 + j])
+        if half in (None, 0):
+            ref = piece(x + 3, y + dy, 0)
+            start(ref, ref, xu_send.at[16 + j], xu_recv.at[16 + j], x_next[0])
+        if half in (None, 1):
+            ref = piece(x + 1, y + dy, 1)
+            start(ref, ref, xd_send.at[16 + j], xd_recv.at[16 + j], x_next[1])
+        to_core(7 + j, below)
+        to_core(11 + j, above)
+
+    def x_far_landed(j):
+        dy, half = PIECES[j]
+        if half in (None, 0):
+            landed(piece(x + 2, y + dy, 0), xu_recv.at[16 + j])
+        if half in (None, 1):
+            landed(piece(x + 2, y + dy, 1), xd_recv.at[16 + j])
+        to_core(15 + j, piece(x + 2, y + dy, half))
+
+    x_landed(0)
+    for i in range(8):
+        recv = xu_recv if i % 2 == 0 else xd_recv
+        landed(z_block(x + 2, ARRIVALS[i], y), recv.at[12 + i // 2])
+    to_core(19, piece(x + 2, y))
+
+    for h in range(2):
+        hop_landed(3, h)
+        frames_landed(1, h)
+        frames_landed(7, h)
+        merge(4, h)
+        hop(4, h)
+    landed(piece(x, y, None, other), core_recv.at[0])
+    for j, (dy, half) in enumerate(PIECES):
+        landed(piece(x, y + dy, half, other), core_recv.at[1 + j])
+    load_chunk(0).start()
+    x_landed(1)
+    x_far_landed(0)
+    x_landed(2)
+    x_far_landed(1)
+    x_landed(3)
+
+    for load in loads[3:]:
+        load.wait()
+    for h in range(2):
+        hop_landed(4, h)
+        frames_landed(0, h)
+        for r in range(RSLOT):
+            source = codes[3 * RSLOT + r] // 64
+            zs, ys = source // NY, lax.rem(source, NY)
+            away = lax.rem(z - zs + NZ, NZ)
+            above = jnp.logical_or(away > 4, jnp.logical_and(away == 4, ys >= 2))
+            at = jnp.where(away == 0, 16 + ys, jnp.where(above, 8 + r, r))
+            xbuf[r, h * HALF : (h + 1) * HALF, :] = last[h][at]
+    x_far_landed(2)
+    lax.fori_loop(0, RSLOT, norm, 0)
+
+    for i, (first, whole) in ((1, (7, 5)), (2, (11, 6))):
+        landed(piece(x + ORDER[i], y, None, other), core_recv.at[whole])
+        for j, (dy, half) in enumerate(PIECES):
+            landed(piece(x + ORDER[i], y + dy, half, other), core_recv.at[first + j])
+        load_chunk(i).start()
+    chunk(0)
+    x_far_landed(3)
+    chunk(1)
+    landed(piece(x + 2, y, None, other), core_recv.at[19])
+    for j, (dy, half) in enumerate(PIECES):
+        landed(piece(x + 2, y + dy, half, other), core_recv.at[15 + j])
+    load_chunk(3).start()
+    chunk(2)
+    chunk(3)
     for i in range(NX):
-        lane = slice(i * CHUNK, (i + 1) * CHUNK)
+        lane = pl.ds(pl.multiple_of(lax.rem(x + ORDER[i], NX) * CHUNK, 128), CHUNK)
         hidden[:, 0:CHUNK] = jnp.dot(
-            act[...], wbuf[i, :, 2 * CHUNK : 3 * CHUNK], preferred_element_type=jnp.float32
+            act[...], wbuf[i, :, :, :, 2 * CHUNK : 3 * CHUNK].reshape(D, CHUNK), preferred_element_type=jnp.float32
         )
+
         ids = lax.broadcasted_iota(jnp.int32, (MAXLEN, CHUNK), 0)
 
         def close(r, carry):
@@ -487,27 +452,66 @@
 
         lax.fori_loop(0, RSLOT, close, 0)
 
-
-def conv_module(codes, xbuf, full, gain, taps, scale, shift):
+    for t in range(NX):
+        same = jnp.logical_and(x == t, keeper == c)
+
+        @pl.when(jnp.logical_not(same))
+        def _():
+            remote(wp.at[t], parts.at[0], part_send.at[t], part_recv.at[0], sibling).wait_send()
+
+    for copy in started:
+        copy.wait_send()
+
+
+def communicate(codes, frames, w_in, w_out, gain, taps, scale, shift):
+    dma = pltpu.SemaphoreType.DMA
     smem = pl.BlockSpec(memory_space=pltpu.SMEM)
     vmem = pl.BlockSpec(memory_space=pltpu.VMEM)
     hbm = pl.BlockSpec(memory_space=pltpu.HBM)
+
+    def slots(n):
+        return [pltpu.VMEM((n, HALF, D), jnp.bfloat16)]
+
     return pl.pallas_call(
-        module_kernel,
-        out_shape=jax.ShapeDtypeStruct((RSLOT, MAXLEN, D), jnp.bfloat16),
-        in_specs=[smem, vmem, hbm, vmem, vmem, vmem, vmem],
-        out_specs=vmem,
+        comm_kernel,
+        out_shape=(
+            jax.ShapeDtypeStruct((RSLOT, MAXLEN, D), jnp.bfloat16),
+            jax.ShapeDtypeStruct((NX, NZ, NY, NC * BLOCK_ROWS, BLOCK_COLS), jnp.bfloat16),
+        ),
+        in_specs=[smem] + [hbm] * 7,
+        out_specs=(vmem, pl.BlockSpec(memory_space=pl.ANY)),
         scratch_shapes=[
-            pltpu.VMEM((NX, D, BLOCK_COLS), jnp.bfloat16),
+            pltpu.VMEM((RSLOT, MAXLEN, D), jnp.bfloat16),
+            pltpu.VMEM((NX, NZ, NY, NC * BLOCK_ROWS, BLOCK_COLS), jnp.bfloat16),
             pltpu.VMEM((RSLOT * MAXLEN, D), jnp.bfloat16),
             pltpu.VMEM((RSLOT * MAXLEN, 2 * CHUNK), jnp.float32),
             pltpu.VMEM((RSLOT, MAXLEN + 2 * PAD, 128), jnp.float32),
             pltpu.VMEM((RSLOT * MAXLEN, D), jnp.bfloat16),
-            pltpu.SemaphoreType.DMA((NX,)),
+            pltpu.VMEM((D,), jnp.float32),
+            pltpu.VMEM((KERNEL, D), jnp.float32),
+            pltpu.VMEM((D,), jnp.float32),
+            pltpu.VMEM((D,), jnp.float32),
+            dma((NX,)),
+            pltpu.VMEM(frames.shape, jnp.bfloat16),
+            pltpu.VMEM(w_in.shape, jnp.bfloat16),
+            pltpu.VMEM(w_out.shape, jnp.bfloat16),
+            pltpu.VMEM((NX, 8, BLOCK_COLS), jnp.bfloat16),
+            pltpu.VMEM((4, 8, BLOCK_COLS), jnp.bfloat16),
+            pltpu.VMEM((BLOCK_ROWS, BLOCK_COLS), jnp.bfloat16),
+            pltpu.VMEM((NZ, NY - 1, MAXLEN, D), jnp.bfloat16),
+            *(slots(4) * 2 + slots(6) * 4 + slots(10) * 4 + slots(12) * 4 + slots(20) * 2 + slots(8) * 8),
+            dma((NZ, NY - 1, 2)), dma((NZ, NY - 1, 2)), dma((4, 2, 2)), dma((4, 2, 2)),
+            dma((4,)), dma((4,)), dma((9,)),
+            dma((4,)), dma((4,)), dma((3,)), dma((3,)),
+            dma((9,)), dma((9,)), dma((9,)), dma((9,)),
+            dma((20,)), dma((20,)), dma((20,)), dma((20,)),
+            dma((20,)), dma((20,)),
         ],
-        compiler_params=pltpu.CompilerParams(vmem_limit_bytes=67043328),
-        name="conv_module",
-    )(codes, xbuf, full, gain, taps, scale, shift)
+        compiler_params=pltpu.CompilerParams(
+            collective_id=0, has_side_effects=True, vmem_limit_bytes=67043328
+        ),
+        name="exchange",
+    )(codes, frames, w_in, w_out, gain, taps, scale, shift)
 
 
 def shards(frames, ln_gain, w_in, depth_kernel, bn_scale, bn_shift, w_out, lengths, destinations, offsets):
@@ -530,11 +534,7 @@
     value = jnp.where(incoming, code_in[None], code_out[None])
     codes = jnp.sum(jnp.where(key == targets, value, 0), axis=(1, 2))
 
-    xbuf, full = communicate(codes, frames[0], w_in, w_out)
-    out = conv_module(
-        codes, xbuf, full.reshape(NX, D, BLOCK_COLS),
-        ln_gain, depth_kernel, bn_scale, bn_shift,
-    )
+    out, _ = communicate(codes, frames[0], w_in, w_out, ln_gain, depth_kernel, bn_scale, bn_shift)
     return out[None]
 
 

time: 110 us -> 106 us (0.964)
  Pallas kernels: 106 us -> 100 us
  local copies, waits for them, and re-layouts: 0.37 us -> 2.44 us
    pallas_call x1 -> x0, Pallas kernels: 14.7 us -> none  [conv_module(): pl.pallas_call(module_kernel, out_shape=jax.ShapeDtypeStruct((RSLOT, MAXL...]
    pallas_call x1, Pallas kernels: 91.6 us -> 100 us  [communicate(): pl.pallas_call(comm_kernel, out_shape=(jax.ShapeDtypeStruct((RSLOT, MAXLE...]
    unnamed x0 -> x1, local copies, waits for them, and re-layouts: none -> 2.06 us
where the time goes in v4:
time: 106 us
  Pallas kernels  100 us (94%)
  other arithmetic  3.14 us (3%)
  local copies, waits for them, and re-layouts  2.44 us (2%)
    pallas_call x1, Pallas kernels, communicate(): pl.pallas_call(comm_kernel, out_shape=(jax.ShapeDtypeStruct((RSLOT, MAXLE...  100 us

profile of v4, /device:TPU:1, one launch (start us, length us, event | category | flops | bytes accessed | tf_op | source)
XLA Modules:
  0.0 105.9 jit_solution(17121276303423707379)
XLA Ops:
  0.0 0.7 broadcast_add_fusion
  0.7 0.1 mul.42
  0.7 0.1 add.69
  0.8 0.8 fusion.3
  1.6 0.1 copy.18
  1.7 0.7 select_bitcast_fusion
  2.4 0.1 copy.19
  2.5 0.1 copy.20
  2.5 1.0 select_reduce_fusion.codes
  3.5 100.3 %exchange.1 = (bf16[8,32,1536]{2,1,0:T(8,128)(2,1)}, bf16[4,8,4,48,1152]{4,3,2,1,0:T(8,128)(2,1)}) custom-call(s32[80]{0:T(128)} %select_reduce_fusion.codes, bf16[24,32,1536]{2,1,0:T(8,128)(2,1)} %bitcast.8, bf16[6,3072]{1,0:T(8,128)(2,1)} %w_in_hbm.1, bf16[6,1536]{1,0:T(8,128)(2,1)} %w_out_hbm.1, f32[1536]{0:T(1024)} %gain_hbm.1, f32[31,1536]{1,0:T(8,128)} %taps_hbm.1, ...), custom_call_target="tpu_custom_call" | custom-call | tf_op jit(solution)/shard_map/exchange/pallas_call | solution.py:475
  103.8 2.1 %copy.22 = bf16[1,8,32,1536]{3,2,1,0:T(8,128)(2,1)} copy(bf16[1,8,32,1536]{3,2,1,0:T(8,128)(2,1)} %bitcast.9) | data formatting | bytes 1572864
  (4 shorter events, 0.0 us)

commit v5 on v4

--- a/solution.py
+++ b/solution.py
@@ -36,7 +36,7 @@
     zu_send, zu_recv, zd_send, zd_recv,
     yu_send, yu_recv, yd_send, yd_recv,
     xu_send, xu_recv, xd_send, xd_recv,
-    core_send, core_recv,
+    core_send, core_recv, lu_send, lu_recv, ld_send, ld_recv,
 ):
     dp = lax.axis_index("dp")
     fs = lax.axis_index("fsdp")
@@ -185,6 +185,34 @@
     def piece(xx, yy, half=None, cc=None):
         rows = slice(None) if half is None else pl.ds(half * 4, 4)
         return full.at[lax.rem(xx, NX), rows, lax.rem(yy, NY), kept(c if cc is None else cc)]
+
+    def most(xx, yy, half=None, cc=None):
+        rows = pl.ds(0, NZ - 1) if half is None else pl.ds(half * 4, 4 - half)
+        return full.at[lax.rem(xx, NX), rows, lax.rem(yy, NY), kept(c if cc is None else cc)]
+
+    def late(xx, yy, cc=None):
+        return full.at[lax.rem(xx, NX), NZ - 1, lax.rem(yy, NY), kept(c if cc is None else cc)]
+
+    def late_start(k):
+        ref = late(x + ORDER[k + 1], y)
+        start(ref, ref, lu_send.at[k], lu_recv.at[k], y_next[0])
+        start(ref, ref, ld_send.at[k], ld_recv.at[k], y_next[1])
+
+    def late_landed(k):
+        below, above = late(x + ORDER[k + 1], y + 3), late(x + ORDER[k + 1], y + 1)
+        landed(below, lu_recv.at[k])
+        landed(above, ld_recv.at[k])
+        if k == 1:
+            start(above, above, ld_send.at[3], ld_recv.at[3], y_next[1])
+        else:
+            start(below, below, lu_send.at[3 + k // 2], lu_recv.at[3 + k // 2], y_next[0])
+        to_core(20 + 3 * k, below)
+        to_core(21 + 3 * k, above)
+
+    def late_far_landed(k):
+        ref = late(x + ORDER[k + 1], y + 2)
+        landed(ref, ld_recv.at[3] if k == 1 else lu_recv.at[3 + k // 2])
+        to_core(22 + 3 * k, ref)
 
     def spread(i):
         dz = ARRIVALS[i]
@@ -321,22 +349,24 @@
     for dz in (1, 7, 0):
         pick_frames(dz)
 
-    def x_start(j, ref):
+    def x_start(j):
+        dy, half = PIECES[j]
+        ref = most(x, y + dy, half)
         start(ref, ref, xu_send.at[8 + j], xu_recv.at[8 + j], x_next[0])
         start(ref, ref, xd_send.at[8 + j], xd_recv.at[8 + j], x_next[1])
-        to_core(1 + j, ref)
+        to_core(1 + j, piece(x, y + dy, half))
 
     for i in range(8):
         landed(z_block(x, ARRIVALS[i], y + 3), yu_recv.at[i])
     ref = piece(x, y + 3, 0)
     start(ref, ref, yu_send.at[8], yu_recv.at[8], y_next[0])
-    x_start(0, piece(x, y + 3))
+    x_start(0)
     for i in range(8):
         landed(z_block(x, ARRIVALS[i], y + 1), yd_recv.at[i])
     ref = piece(x, y + 1, 1)
     start(ref, ref, yd_send.at[8], yd_recv.at[8], y_next[1])
-    x_start(1, piece(x, y + 1))
-    for dz in (1, 7, 0):
+    x_start(1)
+    for dz in (1, 7):
         send_frames(dz)
 
     for i in range(8):
@@ -349,6 +379,9 @@
             start(above, above, xd_send.at[12 + i // 2], xd_recv.at[12 + i // 2], x_next[1])
     to_core(5, piece(x + 3, y))
     to_core(6, piece(x + 1, y))
+    late_start(0)
+    late_start(1)
+    send_frames(0)
 
     for h in range(2):
         hop_landed(2, h)
@@ -358,20 +391,20 @@
         hop(3, h)
 
     landed(piece(x, y + 2, 0), yu_recv.at[8])
-    x_start(2, piece(x, y + 2, 0))
+    x_start(2)
     landed(piece(x, y + 2, 1), yd_recv.at[8])
-    x_start(3, piece(x, y + 2, 1))
+    x_start(3)
 
     def x_landed(j):
         dy, half = PIECES[j]
-        below, above = piece(x + 3, y + dy, half), piece(x + 1, y + dy, half)
+        below, above = most(x + 3, y + dy, half), most(x + 1, y + dy, half)
         landed(below, xu_recv.at[8 + j])
         landed(above, xd_recv.at[8 + j])
         if half in (None, 0):
-            ref = piece(x + 3, y + dy, 0)
+            ref = most(x + 3, y + dy, 0)
             start(ref, ref, xu_send.at[16 + j], xu_recv.at[16 + j], x_next[0])
         if half in (None, 1):
-            ref = piece(x + 1, y + dy, 1)
+            ref = most(x + 1, y + dy, 1)
             start(ref, ref, xd_send.at[16 + j], xd_recv.at[16 + j], x_next[1])
         to_core(7 + j, below)
         to_core(11 + j, above)
@@ -379,16 +412,17 @@
     def x_far_landed(j):
         dy, half = PIECES[j]
         if half in (None, 0):
-            landed(piece(x + 2, y + dy, 0), xu_recv.at[16 + j])
+            landed(most(x + 2, y + dy, 0), xu_recv.at[16 + j])
         if half in (None, 1):
-            landed(piece(x + 2, y + dy, 1), xd_recv.at[16 + j])
-        to_core(15 + j, piece(x + 2, y + dy, half))
+            landed(most(x + 2, y + dy, 1), xd_recv.at[16 + j])
+        to_core(15 + j, most(x + 2, y + dy, half))
 
     x_landed(0)
     for i in range(8):
         recv = xu_recv if i % 2 == 0 else xd_recv
         landed(z_block(x + 2, ARRIVALS[i], y), recv.at[12 + i // 2])
     to_core(19, piece(x + 2, y))
+    late_start(2)
 
     for h in range(2):
         hop_landed(3, h)
@@ -400,10 +434,14 @@
     for j, (dy, half) in enumerate(PIECES):
         landed(piece(x, y + dy, half, other), core_recv.at[1 + j])
     load_chunk(0).start()
+    for k in range(3):
+        late_landed(k)
     x_landed(1)
     x_far_landed(0)
     x_landed(2)
     x_far_landed(1)
+    for k in range(3):
+        late_far_landed(k)
     x_landed(3)
 
     for load in loads[3:]:
@@ -424,14 +462,18 @@
     for i, (first, whole) in ((1, (7, 5)), (2, (11, 6))):
         landed(piece(x + ORDER[i], y, None, other), core_recv.at[whole])
         for j, (dy, half) in enumerate(PIECES):
-            landed(piece(x + ORDER[i], y + dy, half, other), core_recv.at[first + j])
+            landed(most(x + ORDER[i], y + dy, half, other), core_recv.at[first + j])
+        for j, dy in enumerate((3, 1, 2)):
+            landed(late(x + ORDER[i], y + dy, other), core_recv.at[17 + 3 * i + j])
         load_chunk(i).start()
     chunk(0)
     x_far_landed(3)
     chunk(1)
     landed(piece(x + 2, y, None, other), core_recv.at[19])
     for j, (dy, half) in enumerate(PIECES):
-        landed(piece(x + 2, y + dy, half, other), core_recv.at[15 + j])
+        landed(most(x + 2, y + dy, half, other), core_recv.at[15 + j])
+    for j, dy in enumerate((3, 1, 2)):
+        landed(late(x + 2, y + dy, other), core_recv.at[26 + j])
     load_chunk(3).start()
     chunk(2)
     chunk(3)
@@ -505,7 +547,7 @@
             dma((4,)), dma((4,)), dma((3,)), dma((3,)),
             dma((9,)), dma((9,)), dma((9,)), dma((9,)),
             dma((20,)), dma((20,)), dma((20,)), dma((20,)),
-            dma((20,)), dma((20,)),
+            dma((29,)), dma((29,)), dma((5,)), dma((5,)), dma((4,)), dma((4,)),
         ],
         compiler_params=pltpu.CompilerParams(
             collective_id=0, has_side_effects=True, vmem_limit_bytes=67043328

time: 106 us -> 103 us (0.972)
  Pallas kernels: 100 us -> 97 us
    pallas_call x1, Pallas kernels: 100 us -> 97 us  [communicate(): pl.pallas_call(comm_kernel, out_shape=(jax.ShapeDtypeStruct((RSLOT, MAXLE...]
where the time goes in v5:
time: 103 us
  Pallas kernels  97 us (94%)
  other arithmetic  3.14 us (3%)
  local copies, waits for them, and re-layouts  2.44 us (2%)
    pallas_call x1, Pallas kernels, communicate(): pl.pallas_call(comm_kernel, out_shape=(jax.ShapeDtypeStruct((RSLOT, MAXLE...  97 us
    unnamed x1, local copies, waits for them, and re-layouts  2.06 us

profile of v5, /device:TPU:1, one launch (start us, length us, event | category | flops | bytes accessed | tf_op | source)
XLA Modules:
  0.0 102.6 jit_solution(2807300932882851220)
XLA Ops:
  0.0 0.7 broadcast_add_fusion
  0.7 0.1 mul.42
  0.7 0.1 add.69
  0.8 0.8 fusion.3
  1.6 0.1 copy.18
  1.7 0.7 select_bitcast_fusion
  2.4 0.1 copy.19
  2.5 0.1 copy.20
  2.5 1.0 select_reduce_fusion.codes
  3.5 97.0 %exchange.1 = (bf16[8,32,1536]{2,1,0:T(8,128)(2,1)}, bf16[4,8,4,48,1152]{4,3,2,1,0:T(8,128)(2,1)}) custom-call(s32[80]{0:T(128)} %select_reduce_fusion.codes, bf16[24,32,1536]{2,1,0:T(8,128)(2,1)} %bitcast.8, bf16[6,3072]{1,0:T(8,128)(2,1)} %w_in_hbm.1, bf16[6,1536]{1,0:T(8,128)(2,1)} %w_out_hbm.1, f32[1536]{0:T(1024)} %gain_hbm.1, f32[31,1536]{1,0:T(8,128)} %taps_hbm.1, ...), custom_call_target="tpu_custom_call" | custom-call | tf_op jit(solution)/shard_map/exchange/pallas_call | solution.py:517
  100.5 2.1 %copy.22 = bf16[1,8,32,1536]{3,2,1,0:T(8,128)(2,1)} copy(bf16[1,8,32,1536]{3,2,1,0:T(8,128)(2,1)} %bitcast.9) | data formatting | bytes 1572864
  (4 shorter events, 0.0 us)

commit v6 on v5

--- a/solution.py
+++ b/solution.py
@@ -107,7 +107,7 @@
 
     def pick_frames(dz):
         for dy in range(NY):
-            slot = codes[6 * RSLOT + dev(z + dz, y + dy, x, c)[0]]
+            slot = codes[0, 6 * RSLOT + dev(z + dz, y + dy, x, c)[0]]
             if dy:
                 staged[dz, dy - 1] = frames[slot]
             else:
@@ -254,9 +254,9 @@
 
     def merge(step, h):
         for way in range(2):
-            index = (1 if step == 3 else 2) if way == 0 else (4 if step == 3 else 5)
+            index = (1 if step == 3 else 2) if way == 0 else (5 if step == 3 else 4)
             for r in range(RSLOT):
-                source = codes[index * RSLOT + r] // 64
+                source = codes[0, index * RSLOT + r] // 64
                 zs, ys = source // NY, lax.rem(source, NY)
                 away = lax.rem((z - zs if way == 0 else zs - z) + NZ, NZ)
                 if step == 3:
@@ -284,6 +284,11 @@
             ).astype(jnp.bfloat16)
         return carry
 
+    def load_row(dy):
+        rows = lax.rem(y + dy, NY)
+        far_chunk = full.at[lax.rem(x + ORDER[3], NX)]
+        return pltpu.make_async_copy(far_chunk.at[:, rows], wbuf.at[3, :, rows], w_sem.at[3 + dy])
+
     def load_chunk(i):
         return pltpu.make_async_copy(
             full.at[lax.rem(x + ORDER[i], NX)], wbuf.at[i], w_sem.at[i]
@@ -291,7 +296,11 @@
 
     def chunk(i):
         column = lax.rem(x + ORDER[i], NX) * CHUNK
-        load_chunk(i).wait()
+        if i < 3:
+            load_chunk(i).wait()
+        else:
+            for dy in range(NY):
+                load_row(dy).wait()
         hidden[...] = jnp.dot(normed[...], wbuf[i, :, :, :, 0 : 2 * CHUNK].reshape(D, 2 * CHUNK), preferred_element_type=jnp.float32)
         for b in range(CHUNK // 128):
             lane = pl.ds(pl.multiple_of(column + b * 128, 128), 128)
@@ -303,7 +312,7 @@
                 base = pl.multiple_of(r * MAXLEN, MAXLEN)
                 value = hidden[pl.ds(base, MAXLEN), b * 128 : b * 128 + 128]
                 gate = hidden[pl.ds(base, MAXLEN), CHUNK + b * 128 : CHUNK + b * 128 + 128]
-                gated = jnp.where(step_ids < lax.rem(codes[3 * RSLOT + r], 64), value * jax.nn.sigmoid(gate), 0.0)
+                gated = jnp.where(step_ids < lax.rem(codes[0, 3 * RSLOT + r], 64), value * jax.nn.sigmoid(gate), 0.0)
                 window[r, PAD : PAD + MAXLEN, :] = gated
                 total = [None] * 4
                 for first in range(-7, MAXLEN):
@@ -450,7 +459,7 @@
         hop_landed(4, h)
         frames_landed(0, h)
         for r in range(RSLOT):
-            source = codes[3 * RSLOT + r] // 64
+            source = codes[0, 3 * RSLOT + r] // 64
             zs, ys = source // NY, lax.rem(source, NY)
             away = lax.rem(z - zs + NZ, NZ)
             above = jnp.logical_or(away > 4, jnp.logical_and(away == 4, ys >= 2))
@@ -469,13 +478,18 @@
     chunk(0)
     x_far_landed(3)
     chunk(1)
-    landed(piece(x + 2, y, None, other), core_recv.at[19])
-    for j, (dy, half) in enumerate(PIECES):
-        landed(most(x + 2, y + dy, half, other), core_recv.at[15 + j])
     for j, dy in enumerate((3, 1, 2)):
         landed(late(x + 2, y + dy, other), core_recv.at[26 + j])
-    load_chunk(3).start()
+    landed(piece(x + 2, y, None, other), core_recv.at[19])
+    load_row(0).start()
+    for j in range(2):
+        dy = PIECES[j][0]
+        landed(most(x + 2, y + dy, None, other), core_recv.at[15 + j])
+        load_row(dy).start()
     chunk(2)
+    for j in range(2, 4):
+        landed(most(x + 2, y + 2, PIECES[j][1], other), core_recv.at[15 + j])
+    load_row(2).start()
     chunk(3)
     for i in range(NX):
         lane = pl.ds(pl.multiple_of(lax.rem(x + ORDER[i], NX) * CHUNK, 128), CHUNK)
@@ -489,7 +503,7 @@
             mixed = xbuf[r, :, lane].astype(jnp.float32) + hidden[
                 pl.ds(pl.multiple_of(r * MAXLEN, MAXLEN), MAXLEN), 0:CHUNK
             ]
-            out[r, :, lane] = jnp.where(ids < lax.rem(codes[3 * RSLOT + r], 64), mixed, 0.0).astype(jnp.bfloat16)
+            out[r, :, lane] = jnp.where(ids < lax.rem(codes[0, 3 * RSLOT + r], 64), mixed, 0.0).astype(jnp.bfloat16)
             return carry
 
         lax.fori_loop(0, RSLOT, close, 0)
@@ -533,7 +547,7 @@
             pltpu.VMEM((KERNEL, D), jnp.float32),
             pltpu.VMEM((D,), jnp.float32),
             pltpu.VMEM((D,), jnp.float32),
-            dma((NX,)),
+            dma((NX + 3,)),
             pltpu.VMEM(frames.shape, jnp.bfloat16),
             pltpu.VMEM(w_in.shape, jnp.bfloat16),
             pltpu.VMEM(w_out.shape, jnp.bfloat16),
@@ -556,26 +570,45 @@
     )(codes, frames, w_in, w_out, gain, taps, scale, shift)
 
 
+def table_kernel(tab_len, tab_dest, tab_off, codes, rows):
+    dp = lax.axis_index("dp")
+    length, dest = tab_len[...], tab_dest[...]
+    live = length > 0
+    loader = lax.broadcasted_iota(jnp.int32, length.shape, 1)
+    slot = lax.broadcasted_iota(jnp.int32, length.shape, 0).astype(jnp.float32)
+    key_in = jnp.where(live, dest * RSLOT + tab_off[...] // MAXLEN, -1)
+    key_out = jnp.where(jnp.logical_and(live, loader == dp), dest, -1)
+    code = (loader * 64 + length).astype(jnp.float32)
+    rows[...] = jnp.zeros_like(rows)
+    for entry in range(6 * RSLOT + N_DP):
+        if entry < 6 * RSLOT:
+            target = lax.rem(dp // NY + 3 + NZ - entry // RSLOT, NZ) * NY + dp % NY
+            picked = jnp.where(key_in == target * RSLOT + entry % RSLOT, code, 0.0)
+        else:
+            picked = jnp.where(key_out == entry - 6 * RSLOT, slot, 0.0)
+        rows[entry : entry + 1, :] = jnp.sum(picked, axis=0, keepdims=True)
+    total = lax.dot_general(
+        jnp.ones((8, rows.shape[1]), jnp.float32), rows[...], (((1,), (1,)), ((), ())),
+        precision=lax.Precision.HIGHEST, preferred_element_type=jnp.float32,
+    )
+    codes[...] = (total[0:1] + 0.5).astype(jnp.int32)
+
+
+def table(tab_len, tab_dest, tab_off):
+    vmem = pl.BlockSpec(memory_space=pltpu.VMEM)
+    return pl.pallas_call(
+        table_kernel,
+        out_shape=jax.ShapeDtypeStruct((1, 128), jnp.int32),
+        in_specs=[vmem] * 3,
+        out_specs=vmem,
+        scratch_shapes=[pltpu.VMEM((128, tab_len.shape[1]), jnp.float32)],
+        name="table",
+    )(tab_len, tab_dest, tab_off)
+
+
 def shards(frames, ln_gain, w_in, depth_kernel, bn_scale, bn_shift, w_out, lengths, destinations, offsets):
-    dp = lax.axis_index("dp")
     tab_len, tab_dest, tab_off = lengths[0], destinations[0], offsets[0]
-    slots = tab_len.shape[1]
-    peers = jnp.arange(N_DP, dtype=jnp.int32)
-    entry = jnp.arange(6 * RSLOT + N_DP, dtype=jnp.int32)
-    ahead = jnp.array([0, 2, 1, 0, NZ - 2, NZ - 1] + [0] * 4, dtype=jnp.int32)[:, None] * jnp.ones((1, RSLOT), jnp.int32)
-    dests = lax.rem(dp // NY + ahead.reshape(-1), NZ) * NY + dp % NY
-    incoming = entry < 6 * RSLOT
-    targets = jnp.where(incoming, dests * RSLOT + entry % RSLOT, entry - 6 * RSLOT)[:, None, None]
-    incoming = incoming[:, None, None]
-    live = tab_len > 0
-    key_in = jnp.where(live, tab_dest * RSLOT + tab_off // MAXLEN, -1)
-    key_out = jnp.where(live & (peers[:, None] == dp), tab_dest, -1)
-    code_in = peers[:, None] * 64 + tab_len
-    code_out = jnp.broadcast_to(jnp.arange(slots, dtype=jnp.int32)[None, :], tab_len.shape)
-    key = jnp.where(incoming, key_in[None], key_out[None])
-    value = jnp.where(incoming, code_in[None], code_out[None])
-    codes = jnp.sum(jnp.where(key == targets, value, 0), axis=(1, 2))
-
+    codes = table(tab_len.T, tab_dest.T, tab_off.T)
     out, _ = communicate(codes, frames[0], w_in, w_out, ln_gain, depth_kernel, bn_scale, bn_shift)
     return out[None]
 

time: 103 us -> 101 us (0.981)
  other arithmetic: 3.14 us -> 0 us
  Pallas kernels: 97 us -> 98.5 us
    pallas_call x0 -> x1, Pallas kernels: none -> 1.69 us  [table(): pl.pallas_call(table_kernel, out_shape=jax.ShapeDtypeStruct((1, 128), jnp...]
    broadcast_in_dim x2 -> x0, other arithmetic: 1.48 us -> none  [shards(): key = jnp.where(incoming, key_in[None], key_out[None])]
where the time goes in v6:
time: 101 us
  Pallas kernels  98.5 us (98%)
  local copies, waits for them, and re-layouts  2.06 us (2%)
    pallas_call x1, Pallas kernels, communicate(): pl.pallas_call(comm_kernel, out_shape=(jax.ShapeDtypeStruct((RSLOT, MAXLE...  96.8 us
    unnamed x1, local copies, waits for them, and re-layouts  2.06 us

profile of v6, /device:TPU:1, one launch (start us, length us, event | category | flops | bytes accessed | tf_op | source)
XLA Modules:
  0.0 100.6 jit_solution(9709094484748845643)
XLA Ops:
  0.0 1.7 %table.1.codes = s32[1,128]{1,0:T(1,128)} custom-call(s32[24,32]{1,0:T(8,128)} %bitcast.13, s32[24,32]{1,0:T(8,128)} %bitcast.14, s32[24,32]{1,0:T(8,128)} %bitcast.15), custom_call_target="tpu_custom_call" | custom-call | tf_op jit(solution)/shard_map/table/pallas_call | solution.py:599
  1.7 96.8 %exchange.1 = (bf16[8,32,1536]{2,1,0:T(8,128)(2,1)}, bf16[4,8,4,48,1152]{4,3,2,1,0:T(8,128)(2,1)}) custom-call(s32[1,128]{1,0:T(1,128)} %table.1.codes, bf16[24,32,1536]{2,1,0:T(8,128)(2,1)} %bitcast.11, bf16[6,3072]{1,0:T(8,128)(2,1)} %w_in_hbm.1, bf16[6,1536]{1,0:T(8,128)(2,1)} %w_out_hbm.1, f32[1536]{0:T(1024)} %gain_hbm.1, f32[31,1536]{1,0:T(8,128)} %taps_hbm.1, ...), custom_call_target="tpu_custom_call" | custom-call | tf_op jit(solution)/shard_map/exchange/pallas_call | solution.py:531
  98.5 2.1 %copy.12 = bf16[1,8,32,1536]{3,2,1,0:T(8,128)(2,1)} copy(bf16[1,8,32,1536]{3,2,1,0:T(8,128)(2,1)} %bitcast.12) | data formatting | bytes 1572864

commit v7 on v6

--- a/solution.py
+++ b/solution.py
@@ -329,7 +329,7 @@
                     ).astype(jnp.bfloat16)
                 return carry
 
-            lax.fori_loop(0, RSLOT, conv, 0, unroll=4)
+            lax.fori_loop(0, RSLOT, conv, 0, unroll=8)
 
     spread(0)
     for dz in (3, 5):
@@ -506,7 +506,7 @@
             out[r, :, lane] = jnp.where(ids < lax.rem(codes[0, 3 * RSLOT + r], 64), mixed, 0.0).astype(jnp.bfloat16)
             return carry
 
-        lax.fori_loop(0, RSLOT, close, 0)
+        lax.fori_loop(0, RSLOT, close, 0, unroll=4)
 
     for t in range(NX):
         same = jnp.logical_and(x == t, keeper == c)

time: 101 us -> 99.5 us (0.985)
  Pallas kernels: 98.5 us -> 97.1 us
    pallas_call x1, Pallas kernels: 96.8 us -> 95.4 us  [communicate(): pl.pallas_call(comm_kernel, out_shape=(jax.ShapeDtypeStruct((RSLOT, MAXLE...]
where the time goes in v7:
time: 99.5 us; the launch traced here: 99.2 us
  Pallas kernels  97.1 us (98%)
  local copies, waits for them, and re-layouts  2.06 us (2%)
    pallas_call x1, Pallas kernels, communicate(): pl.pallas_call(comm_kernel, out_shape=(jax.ShapeDtypeStruct((RSLOT, MAXLE...  95.4 us
    unnamed x1, local copies, waits for them, and re-layouts  2.06 us

profile of v7, /device:TPU:1, one launch (start us, length us, event | category | flops | bytes accessed | tf_op | source)
XLA Modules:
  0.0 99.2 jit_solution(15041640730222820176)
XLA Ops:
  0.0 1.7 %table.1.codes = s32[1,128]{1,0:T(1,128)} custom-call(s32[24,32]{1,0:T(8,128)} %bitcast.13, s32[24,32]{1,0:T(8,128)} %bitcast.14, s32[24,32]{1,0:T(8,128)} %bitcast.15), custom_call_target="tpu_custom_call" | custom-call | tf_op jit(solution)/shard_map/table/pallas_call | solution.py:599
  1.7 95.4 %exchange.1 = (bf16[8,32,1536]{2,1,0:T(8,128)(2,1)}, bf16[4,8,4,48,1152]{4,3,2,1,0:T(8,128)(2,1)}) custom-call(s32[1,128]{1,0:T(1,128)} %table.1.codes, bf16[24,32,1536]{2,1,0:T(8,128)(2,1)} %bitcast.11, bf16[6,3072]{1,0:T(8,128)(2,1)} %w_in_hbm.1, bf16[6,1536]{1,0:T(8,128)(2,1)} %w_out_hbm.1, f32[1536]{0:T(1024)} %gain_hbm.1, f32[31,1536]{1,0:T(8,128)} %taps_hbm.1, ...), custom_call_target="tpu_custom_call" | custom-call | tf_op jit(solution)/shard_map/exchange/pallas_call | solution.py:531
  97.1 2.1 %copy.12 = bf16[1,8,32,1536]{3,2,1,0:T(8,128)(2,1)} copy(bf16[1,8,32,1536]{3,2,1,0:T(8,128)(2,1)} %bitcast.12) | data formatting | bytes 1572864

commit v8 on v7

--- a/solution.py
+++ b/solution.py
@@ -378,6 +378,13 @@
     for dz in (1, 7):
         send_frames(dz)
 
+    for h in range(2):
+        hop_landed(2, h)
+        frames_landed(2, h)
+        frames_landed(6, h)
+        merge(3, h)
+        hop(3, h)
+
     for i in range(8):
         below, above = z_block(x + 3, ARRIVALS[i], y), z_block(x + 1, ARRIVALS[i], y)
         landed(below, xu_recv.at[i])
@@ -391,13 +398,6 @@
     late_start(0)
     late_start(1)
     send_frames(0)
-
-    for h in range(2):
-        hop_landed(2, h)
-        frames_landed(2, h)
-        frames_landed(6, h)
-        merge(3, h)
-        hop(3, h)
 
     landed(piece(x, y + 2, 0), yu_recv.at[8])
     x_start(2)

time: 99.5 us -> 99.5 us (level)
  no operation moved by 1% of the time
where the time goes in v8:
time: 99.5 us; the launch traced here: 99.2 us
  Pallas kernels  97.1 us (98%)
  local copies, waits for them, and re-layouts  2.06 us (2%)
    pallas_call x1, Pallas kernels, communicate(): pl.pallas_call(comm_kernel, out_shape=(jax.ShapeDtypeStruct((RSLOT, MAXLE...  95.4 us
    unnamed x1, local copies, waits for them, and re-layouts  2.06 us

profile of v8, /device:TPU:1, one launch (start us, length us, event | category | flops | bytes accessed | tf_op | source)
XLA Modules:
  0.0 99.2 jit_solution(10273635165282125633)
XLA Ops:
  0.0 1.7 %table.1.codes = s32[1,128]{1,0:T(1,128)} custom-call(s32[24,32]{1,0:T(8,128)} %bitcast.13, s32[24,32]{1,0:T(8,128)} %bitcast.14, s32[24,32]{1,0:T(8,128)} %bitcast.15), custom_call_target="tpu_custom_call" | custom-call | tf_op jit(solution)/shard_map/table/pallas_call | solution.py:599
  1.7 95.4 %exchange.1 = (bf16[8,32,1536]{2,1,0:T(8,128)(2,1)}, bf16[4,8,4,48,1152]{4,3,2,1,0:T(8,128)(2,1)}) custom-call(s32[1,128]{1,0:T(1,128)} %table.1.codes, bf16[24,32,1536]{2,1,0:T(8,128)(2,1)} %bitcast.11, bf16[6,3072]{1,0:T(8,128)(2,1)} %w_in_hbm.1, bf16[6,1536]{1,0:T(8,128)(2,1)} %w_out_hbm.1, f32[1536]{0:T(1024)} %gain_hbm.1, f32[31,1536]{1,0:T(8,128)} %taps_hbm.1, ...), custom_call_target="tpu_custom_call" | custom-call | tf_op jit(solution)/shard_map/exchange/pallas_call | solution.py:531
  97.1 2.1 %copy.12 = bf16[1,8,32,1536]{3,2,1,0:T(8,128)(2,1)} copy(bf16[1,8,32,1536]{3,2,1,0:T(8,128)(2,1)} %bitcast.12) | data formatting | bytes 1572864
